TPU v7x, 32 devices: a whole 2x2x4 slice. The times are simulated.
32 devices in a mesh: tile: 8 (over z, y), grp: 4 (over x, core).
Axes of the slice: x: 2, y: 2, z: 4, core: 2. Of those that a mesh axis runs over, the one named last changes fastest.
Arguments:
- kelvin_profile: float32 [90, 8, 256], P(None, 'tile'), may hold values from 0.5 to 1.5
- moisture_profile: float32 [90, 8, 256], P(None, 'tile'), may hold values from 0.1 to 3
- spreading_number: float32 [8, 256], P('tile'), may hold values from 0.05 to 0.24
- overhead_angle_measure: float32 [8, 256], P('tile'), may hold values from 0.2 to 1
- illuminated_mask: int32 [8, 256], P('tile'), may hold values 0 or 1
- radiating_tiles: int32 [2048, 1], P('tile'), may hold values from 0 to 7; in each aligned block of 256 rows (0 to 255, 256 to 511, ...) at most 64 rows name the same one
- cloudy_member_factors: float32 [224, 4096], P('grp', 'tile'), may hold values from 0.25 to 2
- arid_opacity_table: float32 [224, 90], P('grp'), may hold values from 0.003 to 0.2
- moisture_attenuation: float32 [224], P('grp'), may hold values from 0.003 to 0.05
- blackbody_share: float32 [224], P('grp'), may hold values from 0.3 to 3
- insolation_per_quadrature: float32 [224], P('grp'), may hold values from 0.3 to 3
Outputs:
- heating: float32 [90, 8, 256], P(None, 'tile')
- temp_next: float32 [90, 8, 256], P(None, 'tile')
- vapour_next: float32 [90, 8, 256], P(None, 'tile')
Inputs may be any that keep to these rules, and one draw needn't show every extreme that they name: `radiating_tiles`: among the columns of one tile no owner is named more than 64 times, a bound that some block reaches.
All inputs are finite; a program needn't handle non-finite values. No bound on the sum of `illuminated_mask` on one device may be relied on, other than what follows from the above.
Results may differ from a plain program's by a relative error of at most 0.00025.
Values sent between devices are 32-bit elements; how exact they have to be, the bound alone decides.
No kernel may reach another device: no remote copies, remote signals or barrier semaphores. Data moves between devices by JAX's collectives and lax.ppermute only.
A program may use at most 64 MiB of HBM per device.

v0:
```python
import math

import jax
import jax.numpy as jnp
from jax import lax
from jax.sharding import PartitionSpec as P

NG = 224


def with_halo(block, sides, width):
    for axis, dim in sides:
        count = lax.axis_size(axis)
        forward = [(i, i + 1) for i in range(count - 1)]
        backward = [(target, source) for source, target in forward]
        low = lax.ppermute(
            lax.slice_in_dim(block, block.shape[dim] - width, None, axis=dim), axis, forward
        )
        high = lax.ppermute(lax.slice_in_dim(block, 0, width, axis=dim), axis, backward)
        block = jnp.concatenate([low, block, high], axis=dim)
    return block


def evaluate_warming(
    kelvin_profile,
    moisture_profile,
    overhead_angle_value,
    illuminated_marker,
    profile_window,
    arid_multiplier,
    moisture_multiplier,
    radiance_share_table,
    sunshine_multiplier,
):
    gpoints, strata_mesh = arid_multiplier.shape
    bundle = math.gcd(gpoints, 4)
    bundles = gpoints // bundle
    lower_mask = (jnp.arange(strata_mesh)[None, :] < jnp.arange(strata_mesh + 1)[:, None]).astype(
        jnp.float32
    )
    upper_mask = 1.0 - lower_mask

    def layer_pass(pieces):
        dry_part, vapour_part, radiance_share_piece, solar_part, sub_part = pieces
        thickness = (
            dry_part[:, :, None]
            + (vapour_part[:, None] * sub_part)[:, None, :] * moisture_profile[None]
        )
        column_depth = jnp.einsum(
            "lk,gkm->glm", lower_mask, thickness, precision=lax.Precision.HIGHEST
        )
        growth = jnp.exp(column_depth)
        damped = jnp.exp(-column_depth)
        infrared_radiance = radiance_share_piece[:, None, None] * kelvin_profile[None]
        downward = damped * jnp.einsum(
            "lk,gkm->glm",
            lower_mask,
            infrared_radiance * growth[:, :strata_mesh] * jnp.expm1(thickness),
            precision=lax.Precision.HIGHEST,
        )
        floor_term = infrared_radiance[:, strata_mesh - 1] * damped[:, strata_mesh]
        upward = growth * (
            floor_term[:, None, :]
            - jnp.einsum(
                "lk,gkm->glm",
                upper_mask,
                infrared_radiance * damped[:, :strata_mesh] * jnp.expm1(-thickness),
                precision=lax.Precision.HIGHEST,
            )
        )
        sunbeam = (
            solar_part[:, None, None]
            * illuminated_marker[None, None, :]
            * jnp.exp(-column_depth / overhead_angle_value[None, None, :])
        )
        fluxes = downward - upward + sunbeam
        return jnp.sum(fluxes[:, :strata_mesh] - fluxes[:, 1:], axis=0)

    spectral = lax.map(
        layer_pass,
        (
            arid_multiplier.reshape(bundles, bundle, strata_mesh),
            moisture_multiplier.reshape(bundles, bundle),
            radiance_share_table.reshape(bundles, bundle),
            sunshine_multiplier.reshape(bundles, bundle),
            profile_window.reshape(bundles, bundle, profile_window.shape[1]),
        ),
    )
    return jnp.sum(spectral, axis=0)


def advance(atmosphere_variables, spreading_number):
    padded = with_halo(atmosphere_variables, (("tile", 2),), 1)
    eastern = jnp.roll(atmosphere_variables, -1, axis=3)
    western = jnp.roll(atmosphere_variables, 1, axis=3)
    return atmosphere_variables + spreading_number * (
        padded[:, :, :-2] + padded[:, :, 2:] + eastern + western - 4.0 * atmosphere_variables
    )


def on_device(
    kelvin_profile,
    moisture_profile,
    spreading_number,
    overhead_angle_measure,
    illuminated_mask,
    radiating_tiles,
    cloudy_member_factors,
    arid_opacity_table,
    moisture_attenuation,
    blackbody_share,
    insolation_per_quadrature,
):
    strata_mesh, parallel_band_sequence, meridian_boxes = kelvin_profile.shape
    atmosphere_variables = jnp.stack([kelvin_profile, moisture_profile])
    for repeat in range(2):
        atmosphere_variables = advance(atmosphere_variables, spreading_number)
    temp_dyn = atmosphere_variables[0]
    vapour_next = atmosphere_variables[1]
    columns = parallel_band_sequence * meridian_boxes
    tile_count = lax.axis_size("tile")
    capacity = cloudy_member_factors.shape[1] // tile_count
    slots = tile_count * capacity
    owner_ids = radiating_tiles[:, 0]
    matches = (owner_ids[:, None] == jnp.arange(tile_count, dtype=jnp.int32)[None, :]).astype(
        jnp.int32
    )
    position = jnp.sum((jnp.cumsum(matches, axis=0) - 1) * matches, axis=1)
    slot_index = owner_ids * capacity + position
    overhead_angle_value = overhead_angle_measure.reshape(columns)
    sunlit_local = overhead_angle_value * illuminated_mask.reshape(columns).astype(jnp.float32)
    local_g = cloudy_member_factors.shape[0]
    blocks = cloudy_member_factors.reshape(local_g, tile_count, capacity)
    homed = lax.all_to_all(blocks, "tile", split_axis=1, concat_axis=1, tiled=True).reshape(
        local_g, slots
    )
    picked_factors = homed[:, slot_index]
    partial_local = evaluate_warming(
        temp_dyn.reshape(strata_mesh, columns),
        vapour_next.reshape(strata_mesh, columns),
        overhead_angle_value,
        sunlit_local,
        picked_factors,
        arid_opacity_table,
        moisture_attenuation,
        blackbody_share,
        insolation_per_quadrature,
    )
    total_heat = lax.psum(partial_local, "grp")
    heating = (total_heat / NG).reshape(strata_mesh, parallel_band_sequence, meridian_boxes)
    return (heating, temp_dyn + heating, vapour_next)


def solution(mesh):
    in_specs = (
        P(None, "tile", None),
        P(None, "tile", None),
        P("tile", None),
        P("tile", None),
        P("tile", None),
        P("tile", None),
        P("grp", "tile"),
        P("grp", None),
        P("grp"),
        P("grp"),
        P("grp"),
    )
    out_specs = (P(None, "tile", None), P(None, "tile", None), P(None, "tile", None))
    return jax.shard_map(
        on_device, mesh=mesh, in_specs=in_specs, out_specs=out_specs, check_vma=False
    )
```

profile of v0, /device:TPU:0, one launch (start us, length us, event | category | flops | bytes accessed | tf_op | source)
XLA Modules:
  0.0 131.5 jit_solution(17511899432500989377)
XLA Ops:
  7.3 1.2 pad_maximum_fusion
  8.5 4.9 %collective-permute-start = (f32[2,90,1,256]{3,2,1,0:T(1,128)S(1)}, f32[2,90,1,256]{3,2,1,0:T(1,128)S(1)}, u32[]{:S(2)}, u32[]{:S(2)}) collective-permute-start(f32[2,90,1,256]{3,2,1,0:T(1,128)S(1)} %pad_maximum_fusion), channel_id=1, source_target_pairs={{0,4},{4,8},{8,12},{12,16},{16,20},{20,24},{24,28},{1,5},{5,9},{9,... | collective-permute-start | bytes 552968 | tf_op jit(solution)/shard_map/ppermute | solution.py:16
  13.4 1.3 collective-permute-start.1
  14.7 1.0 reshape.155
  15.7 0.8 reshape.173
  16.5 7.0 %all-to-all-start = ((f32[8,1,3584]{2,1,0:T(1,128)}), f32[8,1,3584]{2,1,0:T(1,128)S(1)}, u32[]{:S(2)}, u32[]{:S(2)}) async-start(f32[8,1,3584]{2,1,0:T(1,128)} %reshape.173), calls=%async_computation | async-start | bytes 229376 | tf_op jit(solution)/shard_map/all_to_all | solution.py:134
  25.7 1.0 multiply_add_fusion.5
  27.2 3.9 %collective-permute-start.2 = (f32[2,90,1,256]{3,2,1,0:T(1,128)S(1)}, f32[2,90,1,256]{3,2,1,0:T(1,128)S(1)}, u32[]{:S(2)}, u32[]{:S(2)}) collective-permute-start(f32[2,90,1,256]{3,2,1,0:T(1,128)S(1)} %multiply_add_fusion.5), channel_id=1, source_target_pairs={{0,4},{4,8},{8,12},{12,16},{16,20},{20,24},{24,28},{1,5},{5,9},{9,... | collective-permute-start | bytes 552968 | tf_op jit(solution)/shard_map/ppermute | solution.py:16
  31.1 1.3 collective-permute-start.3
  33.2 0.9 reduce.2
  35.2 3.3 %collective-permute-done.3 = f32[2,90,1,256]{3,2,1,0:T(1,128)S(1)} collective-permute-done((f32[2,90,1,256]{3,2,1,0:T(1,128)S(1)}, f32[2,90,1,256]{3,2,1,0:T(1,128)S(1)}, u32[]{:S(2)}, u32[]{:S(2)}) %collective-permute-start.3) | collective-permute-done | bytes 184352 | tf_op jit(solution)/shard_map/ppermute | solution.py:19
  38.6 1.1 multiply_add_fusion.4
  40.5 48.0 %while.12 = (s32[]{:T(128)}, f32[14,90,256]{2,1,0:T(8,128)S(1)}, f32[14,4,90]{2,1,0:T(4,128)}, f32[14,4]{1,0:T(8,128)S(1)}, f32[14,4,256]{2,1,0:T(4,128)S(1)}, /...) while((s32[]{:T(128)}, f32[14,90,256]{2,1,0:T(8,128)S(1)}, ...), condition=%wide.region_5.6_spmd.clone.clone, body=%wide.region_3.5_spmd.clone.clone.sunk | while | flops 304266752 | bytes 6110557 | solution.py:79
  42.9 0.8 fusion.66
  45.6 0.8 fusion.65
  46.4 0.8 fusion.66
  49.8 0.8 fusion.66
  53.2 0.8 fusion.66
  56.6 0.8 fusion.66
  59.3 0.8 fusion.65
  60.1 0.8 fusion.66
  63.5 0.8 fusion.66
  66.9 0.8 fusion.66
  70.3 0.8 fusion.66
  73.0 0.8 fusion.65
  73.8 0.8 fusion.66
  77.2 0.8 fusion.66
  80.6 0.8 fusion.66
  84.0 0.8 fusion.66
  87.5 0.8 fusion.66
  89.2 33.2 %all-reduce.2.cloned.1.call-done = f32[90,256]{1,0:T(8,128)} async-done(((f32[90,256]{1,0:T(8,128)}), f32[90,256]{1,0:T(8,128)}) %all-reduce.2.cloned.1.call-update) | async-done | bytes 92176 | tf_op jit(solution)/shard_map/psum | solution.py:149
  122.3 0.9 bitcast_add_fusion
  (233 shorter events, 39.7 us)
Async XLA Ops:
  7.2 16.4 %copy-start = (f32[90,1,256]{2,1,0:T(1,128)S(1)}, f32[90,1,256]{2,1,0:T(1,128)}, u32[]{:S(2)}) copy-start(f32[90,1,256]{2,1,0:T(1,128)} %param.14) | copy-start | bytes 276484
  7.2 16.4 %copy-start.1 = (f32[90,1,256]{2,1,0:T(1,128)S(1)}, f32[90,1,256]{2,1,0:T(1,128)}, u32[]{:S(2)}) copy-start(f32[90,1,256]{2,1,0:T(1,128)} %param.13) | copy-start | bytes 276484
  7.2 17.2 %copy-start.2 = (s32[256,1]{0,1:T(1,128)S(1)}, s32[256,1]{0,1:T(1,128)}, u32[]{:S(2)}) copy-start(s32[256,1]{0,1:T(1,128)} %param.18) | copy-start | bytes 3076
  7.2 18.2 %copy-start.6 = (f32[56]{0:T(128)S(1)}, f32[56]{0:T(128)}, u32[]{:S(2)}) copy-start(f32[56]{0:T(128)} %param.21) | copy-start | bytes 676
  7.2 18.3 %copy-start.7 = (f32[56]{0:T(128)S(1)}, f32[56]{0:T(128)}, u32[]{:S(2)}) copy-start(f32[56]{0:T(128)} %param.22) | copy-start | bytes 676
  7.2 18.3 %copy-start.8 = (f32[56]{0:T(128)S(1)}, f32[56]{0:T(128)}, u32[]{:S(2)}) copy-start(f32[56]{0:T(128)} %param.23) | copy-start | bytes 676
  7.2 18.4 %copy-start.4 = (s32[1,256]{1,0:T(1,128)S(1)}, s32[1,256]{1,0:T(1,128)}, u32[]{:S(2)}) copy-start(s32[1,256]{1,0:T(1,128)} %param.17) | copy-start | bytes 3076
  7.2 18.4 %copy-start.5 = (f32[1,256]{1,0:T(1,128)S(1)}, f32[1,256]{1,0:T(1,128)}, u32[]{:S(2)}) copy-start(f32[1,256]{1,0:T(1,128)} %param.16) | copy-start | bytes 3076
  7.2 18.5 %copy-start.3 = (f32[1,256]{1,0:T(1,128)S(1)}, f32[1,256]{1,0:T(1,128)}, u32[]{:S(2)}) copy-start(f32[1,256]{1,0:T(1,128)} %param.15) | copy-start | bytes 3076
  8.5 17.2 %collective-permute-start = (f32[2,90,1,256]{3,2,1,0:T(1,128)S(1)}, f32[2,90,1,256]{3,2,1,0:T(1,128)S(1)}, u32[]{:S(2)}, u32[]{:S(2)}) collective-permute-start(f32[2,90,1,256]{3,2,1,0:T(1,128)S(1)} %pad_maximum_fusion), channel_id=1, source_target_pairs={{0,4},{4,8},{8,12},{12,16},{16,20},{20,24},{24,28},{1,5},{5,9},{9,... | collective-permute-start | bytes 552968 | tf_op jit(solution)/shard_map/ppermute | solution.py:16
  13.4 12.3 %collective-permute-start.1 = (f32[2,90,1,256]{3,2,1,0:T(1,128)S(1)}, f32[2,90,1,256]{3,2,1,0:T(1,128)S(1)}, u32[]{:S(2)}, u32[]{:S(2)}) collective-permute-start(f32[2,90,1,256]{3,2,1,0:T(1,128)S(1)} %pad_maximum_fusion), channel_id=1, source_target_pairs={{4,0},{8,4},{12,8},{16,12},{20,16},{24,20},{28,24},{5,1},{9,5},{13... | collective-permute-start | bytes 552968 | tf_op jit(solution)/shard_map/ppermute | solution.py:19
  16.5 16.1 %all-to-all-start = ((f32[8,1,3584]{2,1,0:T(1,128)}), f32[8,1,3584]{2,1,0:T(1,128)S(1)}, u32[]{:S(2)}, u32[]{:S(2)}) async-start(f32[8,1,3584]{2,1,0:T(1,128)} %reshape.173), calls=%async_computation | async-start | bytes 229376 | tf_op jit(solution)/shard_map/all_to_all | solution.py:134
  23.5 98.8 %all-reduce.2.cloned.1.call-start = ((), (), s32[]{:S(2)}) async-start(), calls=%async_computation.1 | async-start | bytes 196608 | tf_op jit(solution)/shard_map/psum | solution.py:149
  27.2 8.0 %collective-permute-start.2 = (f32[2,90,1,256]{3,2,1,0:T(1,128)S(1)}, f32[2,90,1,256]{3,2,1,0:T(1,128)S(1)}, u32[]{:S(2)}, u32[]{:S(2)}) collective-permute-start(f32[2,90,1,256]{3,2,1,0:T(1,128)S(1)} %multiply_add_fusion.5), channel_id=1, source_target_pairs={{0,4},{4,8},{8,12},{12,16},{16,20},{20,24},{24,28},{1,5},{5,9},{9,... | collective-permute-start | bytes 552968 | tf_op jit(solution)/shard_map/ppermute | solution.py:16
  31.1 7.4 %collective-permute-start.3 = (f32[2,90,1,256]{3,2,1,0:T(1,128)S(1)}, f32[2,90,1,256]{3,2,1,0:T(1,128)S(1)}, u32[]{:S(2)}, u32[]{:S(2)}) collective-permute-start(f32[2,90,1,256]{3,2,1,0:T(1,128)S(1)} %multiply_add_fusion.5), channel_id=1, source_target_pairs={{4,0},{8,4},{12,8},{16,12},{20,16},{24,20},{28,24},{5,1},{9,5},{13... | collective-permute-start | bytes 552968 | tf_op jit(solution)/shard_map/ppermute | solution.py:19
Sparse Core Ops, SparseCore 0:
  89.3 32.9 all-reduce.1
where the time goes:
time: 132 us; the launch traced here: 131 us
  waiting for transfers between devices  36.5 us (28%)
  matrix products  31.3 us (24%)
  starting transfers between devices  18.4 us (14%)
  local copies, waits for them, and re-layouts  17.1 us (13%)
  between operations  14.4 us (11%)
  other arithmetic  12.2 us (9%)
  loops' own time  1.46 us (1%)
    psum x1, waiting for transfers between devices, on_device(): total_heat = lax.psum(partial_local, 'grp')  33.2 us
    dot_general x14, matrix products, layer_pass(): jnp.einsum('lk,gkm->glm', lower_mask, infrared_radiance * growth[:, :stra...  11.8 us
    dot_general x14, matrix products, layer_pass(): jnp.einsum('lk,gkm->glm', upper_mask, infrared_radiance * damped[:, :stra...  11.2 us
    add x14, local copies, waits for them, and re-layouts, layer_pass(): dry_part[:, :, None]  9.56 us
    ppermute x2, starting transfers between devices, with_halo(): lax.ppermute(lax.slice_in_dim(block, block.shape[dim] - width, None, axis...  8.8 us
    dot_general x14, matrix products, layer_pass(): jnp.einsum('lk,gkm->glm', lower_mask, thickness, precision=lax.Precision....  8.39 us
    all_to_all x1, starting transfers between devices, on_device(): lax.all_to_all(blocks, 'tile', split_axis=1, concat_axis=1, tiled=True)  6.96 us
    ppermute x2, waiting for transfers between devices, with_halo(): lax.ppermute(lax.slice_in_dim(block, 0, width, axis=dim), axis, backward)  3.35 us
  transfers between devices with their start and end apart: 6, of which 2 were waited for; matrix products, arithmetic and copies ran while one was open for 6% of the time, Pallas kernels for 0%

commit v1 on v0

v1 whole, which is shorter than its diff:
```python
import functools
import math

import jax
import jax.numpy as jnp
from jax import lax
from jax.experimental import pallas as pl
from jax.experimental.pallas import tpu as pltpu
from jax.sharding import PartitionSpec as P

LOG2E = math.log2(math.e)
VM = pl.BlockSpec(memory_space=pltpu.VMEM)


def kernel_call(body, out_shapes, scratch=(), flops=1 << 22, name=None):
    return pl.pallas_call(
        body,
        out_shape=[jax.ShapeDtypeStruct(s, jnp.float32) for s in out_shapes],
        out_specs=[VM] * len(out_shapes),
        scratch_shapes=list(scratch),
        compiler_params=pltpu.CompilerParams(vmem_limit_bytes=24 << 20),
        cost_estimate=pl.CostEstimate(flops=flops, bytes_accessed=1 << 21, transcendentals=0),
        name=name,
    )


def split3(x):
    high = x.astype(jnp.bfloat16)
    rest = x - high.astype(jnp.float32)
    middle = rest.astype(jnp.bfloat16)
    low = (rest - middle.astype(jnp.float32)).astype(jnp.bfloat16)
    return high, middle, low


def column_of(row):
    n = row.shape[1]
    r = lax.broadcasted_iota(jnp.int32, (n, n), 0)
    c = lax.broadcasted_iota(jnp.int32, (n, n), 1)
    return jnp.sum(jnp.where(r == c, jnp.broadcast_to(row, (n, n)), 0.0), axis=1, keepdims=True)


def around(v):
    width = v.shape[1]
    return pltpu.roll(v, width - 1, 1) + pltpu.roll(v, 1, 1) - 4.0 * v


def pack_kernel(cap, kelvin, moisture, spread, factors, fields, blocks):
    levels = kelvin.shape[0]
    tiles, rows, _ = blocks.shape
    top = factors.shape[0] - rows
    lane = lax.broadcasted_iota(jnp.int32, (rows, 2 * cap), 1)
    for pair in range(tiles // 2):
        first = factors[0:rows, pair * 2 * cap : (pair + 1) * 2 * cap]
        second = factors[top : top + rows, pair * 2 * cap : (pair + 1) * 2 * cap]
        blocks[2 * pair] = jnp.where(lane < cap, first, pltpu.roll(second, cap, 1))
        blocks[2 * pair + 1] = jnp.where(lane < cap, pltpu.roll(first, cap, 1), second)
    stack_fields(levels, kelvin, moisture, spread, fields)


def stack_fields(levels, kelvin, moisture, spread, fields):
    for l in range(levels):
        fields[l : l + 1, :] = kelvin[l]
        fields[levels + l : levels + l + 1, :] = moisture[l]
    fields[2 * levels : 2 * levels + 1, :] = spread[...]
    rest = fields.shape[0] - 2 * levels - 1
    if rest:
        fields[2 * levels + 1 :, :] = jnp.zeros((rest, fields.shape[1]), jnp.float32)


def fields_kernel(kelvin, moisture, spread, fields):
    stack_fields(kelvin.shape[0], kelvin, moisture, spread, fields)


def gather_kernel(cap, tiles, packed, levels, homed, owners, vapour, arid, fields, weights, dry, base):
    columns = owners.shape[1]
    gpoints = arid.shape[0]
    owner = owners[...]
    matches = lax.broadcasted_iota(jnp.int32, (tiles, columns), 0) == owner
    member = matches.astype(jnp.float32)
    r = lax.broadcasted_iota(jnp.int32, (columns, columns), 0)
    c = lax.broadcasted_iota(jnp.int32, (columns, columns), 1)
    earlier = (r < c).astype(jnp.float32).astype(jnp.bfloat16)
    counts = jnp.dot(member.astype(jnp.bfloat16), earlier, preferred_element_type=jnp.float32)
    rank = jnp.sum(jnp.where(matches, counts, 0.0), axis=0, keepdims=True)
    slot = owner * cap + rank.astype(jnp.int32)
    choice = (lax.broadcasted_iota(jnp.int32, (tiles * cap, columns), 0) == slot).astype(jnp.float32)
    choice = choice.astype(jnp.bfloat16)
    if packed:
        rows = homed.shape[1]
        lane = lax.broadcasted_iota(jnp.int32, (rows, 2 * cap), 1)
        lower, upper = [], []
        for pair in range(tiles // 2):
            first, second = homed[2 * pair], homed[2 * pair + 1]
            lower.append(jnp.where(lane < cap, first, pltpu.roll(second, cap, 1)))
            upper.append(jnp.where(lane < cap, pltpu.roll(first, cap, 1), second))
        lower = jnp.concatenate(lower, axis=1)
        upper = jnp.concatenate(upper, axis=1)[2 * rows - gpoints :]
        table = jnp.concatenate([lower, upper], axis=0)
    else:
        table = homed[...]
    picked = 0.0
    for part in split3(table):
        picked = picked + jnp.dot(part, choice, preferred_element_type=jnp.float32)
    weights[...] = picked * (column_of(vapour[...]) * -LOG2E)
    for l in range(levels):
        dry[l] = jnp.broadcast_to(arid[:, l : l + 1] * -LOG2E, (gpoints, dry.shape[2]))
    f = fields[...]
    spread = fields[2 * levels : 2 * levels + 1, :]
    f = f + spread * around(f)
    base[...] = f + spread * around(f)


def side_kernel(levels, fields, near, far, base, share, total):
    spread = fields[2 * levels : 2 * levels + 1, :]
    near_spread = near[2 * levels : 2 * levels + 1, :]
    f = near[...]
    near_next = f + near_spread * (far[...] + fields[...] + around(f))
    v = spread * f
    part = v + spread * (around(v) + near_next)
    share[...] = part
    total[...] = base[...] + part


def radiation_kernel(
    levels, gpoints, base, share, weights, dry, angle, lit, black, solar, part, vapour, temp, rest, sums
):
    width = base.shape[1]
    blocks = gpoints // 8
    f = base[...] + share[...]
    for l in range(levels):
        temp[l] = f[l : l + 1]
        vapour[l] = f[levels + l : levels + l + 1]
    black_column = jnp.broadcast_to(column_of(black[...]), (gpoints, 128))
    solar_column = jnp.broadcast_to(column_of(solar[...]), (gpoints, 128))
    unroll = max(u for u in range(1, 11) if levels % u == 0)
    for half in range(width // 128):
        at = slice(half * 128, (half + 1) * 128)
        mu = jnp.broadcast_to(angle[:, at], (8, 128))
        inverse = 1.0 / mu
        marker = mu * jnp.broadcast_to(lit[:, at].astype(jnp.float32), (8, 128))
        share_of = [black_column[8 * b : 8 * b + 8] for b in range(blocks)]
        weight = [weights[8 * b : 8 * b + 8, at] for b in range(blocks)]
        beams = tuple(solar_column[8 * b : 8 * b + 8] * marker for b in range(blocks))
        zero = tuple(jnp.zeros((8, 128), jnp.float32) for b in range(blocks))

        def down_level(l, carry):
            down, beam = carry
            warm = jnp.broadcast_to(temp[l, :, at], (8, 128))
            wet = jnp.broadcast_to(vapour[l, :, at], (8, 128))
            new_down, new_beam, acc = [], [], None
            for b in range(blocks):
                tau = dry[l, 8 * b : 8 * b + 8, :] + weight[b] * wet
                lost = 1.0 - jnp.exp2(tau)
                rest[l, 8 * b : 8 * b + 8, at] = lost
                step = lost * (down[b] - share_of[b] * warm)
                after = beam[b] * jnp.exp2(tau * inverse)
                net = step + (beam[b] - after)
                acc = net if acc is None else acc + net
                new_down.append(down[b] - step)
                new_beam.append(after)
            sums[half, pl.ds(pl.multiple_of(l * 8, 8), 8), :] = acc
            return tuple(new_down), tuple(new_beam)

        def up_level(i, up):
            l = levels - 1 - i
            warm = jnp.broadcast_to(temp[l, :, at], (8, 128))
            new_up, acc = [], None
            for b in range(blocks):
                step = rest[l, 8 * b : 8 * b + 8, at] * (share_of[b] * warm - up[b])
                acc = step if acc is None else acc + step
                new_up.append(up[b] + step)
            where = pl.ds(pl.multiple_of(l * 8, 8), 8)
            sums[half, where, :] = sums[half, where, :] - acc
            return tuple(new_up)

        lax.fori_loop(0, levels, down_level, (zero, beams), unroll=unroll)
        floor = jnp.broadcast_to(temp[levels - 1, :, at], (8, 128))
        lax.fori_loop(0, levels, up_level, tuple(s * floor for s in share_of), unroll=unroll)
    for half in range(width // 128):
        at = slice(half * 128, (half + 1) * 128)
        total = sums[half, pl.ds(0, levels, stride=8), :]
        for s in range(1, 8):
            total = total + sums[half, pl.ds(s, levels, stride=8), :]
        part[:, at] = total


def final_kernel(scale, one, two, temp, heating, temp_next):
    levels = one.shape[0]
    heat = (one[...] + two[...]) * scale
    for l in range(levels):
        heating[l] = heat[l : l + 1]
        temp_next[l] = temp[l] + heat[l : l + 1]


def on_device(
    n_tile,
    n_grp,
    kelvin,
    moisture,
    spreading_number,
    angle,
    lit,
    owners,
    factors,
    arid,
    vapour_absorption,
    black,
    solar,
):
    levels, rows, width = kelvin.shape
    gpoints, slots = factors.shape
    cap = slots // n_tile
    total_g = gpoints * n_grp
    if rows != 1 or n_grp & (n_grp - 1) or n_grp < 2 or gpoints % 8 or width % 128:
        raise ValueError("unsupported shapes")
    stacked = -(-(2 * levels + 1) // 8) * 8
    packed = 2 * cap == 128 and gpoints % 16 == 8 and n_tile % 2 == 0
    if packed:
        half = (gpoints + 8) // 2
        fields, blocks = kernel_call(
            functools.partial(pack_kernel, cap), [(stacked, width), (n_tile, half, 128)], name="pack"
        )(kelvin, moisture, spreading_number, factors)
        homed = lax.all_to_all(blocks, "tile", split_axis=0, concat_axis=0, tiled=True)
    else:
        (fields,) = kernel_call(fields_kernel, [(stacked, width)], name="pack")(
            kelvin, moisture, spreading_number
        )
        blocks = factors.reshape(gpoints, n_tile, cap)
        homed = lax.all_to_all(blocks, "tile", split_axis=1, concat_axis=1, tiled=True)
        homed = homed.reshape(gpoints, slots)

    def from_side(distance):
        pairs = []
        for t in range(n_tile):
            for g in range(n_grp):
                s = t - distance if g % 2 == 0 else t + distance
                if 0 <= s < n_tile:
                    pairs.append((s * n_grp + g, t * n_grp + g))
        return lax.ppermute(fields, ("tile", "grp"), pairs)

    def swapped(x, bit):
        return lax.ppermute(x, "grp", [(i, i ^ bit) for i in range(n_grp)])

    near = from_side(1)
    far = from_side(2)
    weights, dry, base = kernel_call(
        functools.partial(gather_kernel, cap, n_tile, packed, levels),
        [(gpoints, width), (levels, gpoints, 128), (stacked, width)],
        name="gather",
    )(homed, owners.reshape(1, width), vapour_absorption.reshape(1, gpoints), arid, fields)
    share, mine = kernel_call(
        functools.partial(side_kernel, levels), [(stacked, width)] * 2, name="side"
    )(fields, near, far, base)
    other = swapped(share, 1)
    part, vapour_next, temp = kernel_call(
        functools.partial(radiation_kernel, levels, gpoints),
        [(levels, width), (levels, 1, width), (levels, 1, width)],
        scratch=[
            pltpu.VMEM((levels, gpoints, width), jnp.float32),
            pltpu.VMEM((width // 128, levels * 8, 128), jnp.float32),
        ],
        name="radiation",
    )(mine, other, weights, dry, angle, lit, black.reshape(1, gpoints), solar.reshape(1, gpoints))
    bit = 1
    while 2 * bit < n_grp:
        part = part + swapped(part, bit)
        bit *= 2
    heating, temp_next = kernel_call(
        functools.partial(final_kernel, 1.0 / total_g), [(levels, 1, width)] * 2, name="final"
    )(part, swapped(part, bit), temp)
    return heating, temp_next, vapour_next


def solution(mesh):
    in_specs = (
        P(None, "tile", None),
        P(None, "tile", None),
        P("tile", None),
        P("tile", None),
        P("tile", None),
        P("tile", None),
        P("grp", "tile"),
        P("grp", None),
        P("grp"),
        P("grp"),
        P("grp"),
    )
    out_specs = (P(None, "tile", None), P(None, "tile", None), P(None, "tile", None))
    body = functools.partial(on_device, mesh.shape["tile"], mesh.shape["grp"])
    return jax.shard_map(body, mesh=mesh, in_specs=in_specs, out_specs=out_specs, check_vma=False)
```

time: 132 us -> 39.3 us (0.30)
  matrix products: 31.3 us -> 0 us
  waiting for transfers between devices: 36.5 us -> 6.31 us
  between operations: 14.4 us -> 0.71 us
  other arithmetic: 12.2 us -> 0.01 us
  local copies, waits for them, and re-layouts: 17.1 us -> 8.1 us
  Pallas kernels: 0 us -> 7.3 us
  starting transfers between devices: 18.4 us -> 16.4 us
  loops' own time: 1.46 us -> 0 us
    psum x1 -> x0, waiting for transfers between devices: 33.2 us -> none  [on_device(): total_heat = lax.psum(partial_local, 'grp')]
    dot_general x42 -> x0, matrix products: 31.3 us -> none  [the longest x14 11.8 us: layer_pass(): jnp.einsum('lk,gkm->glm', lower_mask, infrared_radiance * growth[:, :stra...]
    add x15 -> x0, local copies, waits for them, and re-layouts: 10.3 us -> none  [the longest x14 9.56 us: layer_pass(): dry_part[:, :, None]]
    pallas_call x0 -> x5, Pallas kernels: none -> 7.3 us  [the longest x1 4.27 us: on_device(): kernel_call(functools.partial(radiation_kernel, levels, gpoints), [(level...]
    unnamed x22, local copies, waits for them, and re-layouts: 0.97 us -> 8.1 us
    add x3 -> x1, other arithmetic: 2.99 us -> 0.01 us  [on_device(): part = part + swapped(part, bit)]
    another operation x5 -> x0, other arithmetic: 2.63 us -> none  [the longest x3 2 us: on_device(): atmosphere_variables = jnp.stack([kelvin_profile, moisture_profile])]
    ppermute x4 -> x5, waiting for transfers between devices: 3.36 us -> 5.94 us  [the longest x3 5.94 us: swapped(): return lax.ppermute(x, 'grp', [(i, i ^ bit) for i in range(n_grp)])]
  transfers between devices with their start and end apart: 6 -> 6, of which waited for: 2 -> 4; matrix products, arithmetic and copies ran while one was open for 6% -> 0% of each run, Pallas kernels for 0% -> 3%
where the time goes in v1:
time: 39.3 us; the launch traced here: 38.8 us
  starting transfers between devices  16.4 us (42%)
  local copies, waits for them, and re-layouts  8.1 us (21%)
  Pallas kernels  7.3 us (19%)
  waiting for transfers between devices  6.31 us (16%)
  between operations  0.71 us (2%)
    unnamed x22, local copies, waits for them, and re-layouts  8.1 us
    all_to_all x1, starting transfers between devices, on_device(): lax.all_to_all(blocks, 'tile', split_axis=0, concat_axis=0, tiled=True)  7.31 us
    ppermute x2, starting transfers between devices, from_side(): return lax.ppermute(fields, ('tile', 'grp'), pairs)  7.3 us
    ppermute x3, waiting for transfers between devices, swapped(): return lax.ppermute(x, 'grp', [(i, i ^ bit) for i in range(n_grp)])  5.94 us
    pallas_call x1, Pallas kernels, on_device(): kernel_call(functools.partial(radiation_kernel, levels, gpoints), [(level...  4.27 us
    ppermute x3, starting transfers between devices, swapped(): return lax.ppermute(x, 'grp', [(i, i ^ bit) for i in range(n_grp)])  1.77 us
    pallas_call x1, Pallas kernels, on_device(): kernel_call(functools.partial(gather_kernel, cap, n_tile, packed, levels)...  1.22 us
  transfers between devices with their start and end apart: 6, of which 4 were waited for; matrix products, arithmetic and copies ran while one was open for 0% of the time, Pallas kernels for 3%

profile of v1, /device:TPU:0, one launch (start us, length us, event | category | flops | bytes accessed | tf_op | source)
XLA Modules:
  0.0 38.8 jit_solution(240830226386433153)
XLA Ops:
  0.6 0.0 copy-start
  0.6 0.9 %copy-done = f32[56,512]{1,0:T(8,128)S(1)} copy-done((f32[56,512]{1,0:T(8,128)S(1)}, f32[56,512]{1,0:T(8,128)}, u32[]{:S(2)}) %copy-start) | copy-done | bytes 114712
  1.5 0.0 copy-start.1
  1.5 0.9 %copy-done.1 = f32[90,1,256]{2,1,0:T(1,128)S(1)} copy-done((f32[90,1,256]{2,1,0:T(1,128)S(1)}, f32[90,1,256]{2,1,0:T(1,128)}, u32[]{:S(2)}) %copy-start.1) | copy-done | bytes 92184
  2.4 0.0 copy-start.2
  2.4 0.9 %copy-done.2 = f32[90,1,256]{2,1,0:T(1,128)S(1)} copy-done((f32[90,1,256]{2,1,0:T(1,128)S(1)}, f32[90,1,256]{2,1,0:T(1,128)}, u32[]{:S(2)}) %copy-start.2) | copy-done | bytes 92184
  3.3 0.0 copy-start.4
  3.3 0.7 %copy-done.4 = f32[1,256]{1,0:T(1,128)S(1)} copy-done((f32[1,256]{1,0:T(1,128)S(1)}, f32[1,256]{1,0:T(1,128)}, u32[]{:S(2)}) %copy-start.4) | copy-done | bytes 1048
  4.0 0.8 %pack.1 = (f32[184,256]{1,0:T(8,128)S(1)}, f32[8,32,128]{2,1,0:T(8,128)}) custom-call(f32[90,1,256]{2,1,0:T(1,128)S(1)} %copy-done.1, f32[90,1,256]{2,1,0:T(1,128)S(1)} %copy-done.2, f32[1,256]{1,0:T(1,128)S(1)} %copy-done.4, f32[56,512]{1,0:T(8,128)S(1)} %copy-done), custom_call_target="tpu_custom_call" | custom-call | flops 4194304 | bytes 2097152 | tf_op jit(solution)/shard_map/pack/pallas_call | solution.py:220
  4.8 7.3 %all-to-all-start = ((f32[8,32,128]{2,1,0:T(8,128)}), f32[8,32,128]{2,1,0:T(8,128)S(1)}, u32[]{:S(2)}, u32[]{:S(2)}) async-start(f32[8,32,128]{2,1,0:T(8,128)} %get-tuple-element.16), calls=%async_computation | async-start | bytes 262144 | tf_op jit(solution)/shard_map/all_to_all | solution.py:223
  12.1 3.9 %collective-permute-start.1 = (f32[184,256]{1,0:T(8,128)S(1)}, f32[184,256]{1,0:T(8,128)S(1)}, u32[]{:S(2)}, u32[]{:S(2)}) collective-permute-start(f32[184,256]{1,0:T(8,128)S(1)} %get-tuple-element.15.fields), channel_id=1, source_target_pairs={{9,1},{11,3},{13,5},{15,7},{0,8},{17,9},{2,10},{19,11},{4,12},{21,... | collective-permute-start | bytes 565256 | tf_op jit(solution)/shard_map/ppermute | solution.py:239
  16.0 3.4 %collective-permute-start = (f32[184,256]{1,0:T(8,128)S(1)}, f32[184,256]{1,0:T(8,128)S(1)}, u32[]{:S(2)}, u32[]{:S(2)}) collective-permute-start(f32[184,256]{1,0:T(8,128)S(1)} %get-tuple-element.15.fields), channel_id=1, source_target_pairs={{5,1},{7,3},{0,4},{9,5},{2,6},{11,7},{4,8},{13,9},{6,10},{15,11},{... | collective-permute-start | bytes 565256 | tf_op jit(solution)/shard_map/ppermute | solution.py:239
  19.4 0.4 all-to-all-done.homed
  19.7 0.7 %copy-done.3 = f32[56,90]{1,0:T(8,128)S(1)} copy-done((f32[56,90]{1,0:T(8,128)S(1)}, f32[56,90]{1,0:T(8,128)}, u32[]{:S(2)}) %copy-start.3) | copy-done | bytes 20184
  20.5 0.7 %copy-done.5 = s32[256,1]{0,1:T(1,128)S(1)} copy-done((s32[256,1]{0,1:T(1,128)S(1)}, s32[256,1]{0,1:T(1,128)}, u32[]{:S(2)}) %copy-start.5) | copy-done | bytes 1048
  21.2 0.7 %copy-done.8 = f32[56]{0:T(128)S(1)} copy-done((f32[56]{0:T(128)S(1)}, f32[56]{0:T(128)}, u32[]{:S(2)}) %copy-start.8) | copy-done | bytes 248
  21.8 1.2 %gather.1 = (f32[56,256]{1,0:T(8,128)S(1)}, f32[90,56,128]{2,1,0:T(8,128)S(1)}, f32[184,256]{1,0:T(8,128)S(1)}) custom-call(f32[8,32,128]{2,1,0:T(8,128)S(1)} %all-to-all-done.homed, s32[1,256]{1,0:T(1,128)S(1)} %bitcast.4, f32[1,56]{1,0:T(1,128)S(1)} %bitcast.5, f32[56,90]{1,0:T(8,128)S(1)} %copy-done.3, f32[184,256]{1,0:T(8,128)S(1)} %get-tuple-element.15.fields), custom_call_target="tpu_custom_call" | custom-call | flops 4194304 | bytes 2097152 | tf_op jit(solution)/shard_map/gather/pallas_call | solution.py:246
  23.1 0.0 collective-permute-done.1.far
  23.1 0.0 collective-permute-done.near
  23.1 0.3 side.1
  23.4 0.1 collective-permute-start.2
  23.5 1.4 %collective-permute-done.2.share = f32[184,256]{1,0:T(8,128)S(1)} collective-permute-done((f32[184,256]{1,0:T(8,128)S(1)}, f32[184,256]{1,0:T(8,128)S(1)}, u32[]{:S(2)}, u32[]{:S(2)}) %collective-permute-start.2) | collective-permute-done | bytes 188448 | tf_op jit(solution)/shard_map/ppermute | solution.py:242
  24.9 0.7 %copy-done.6 = f32[1,256]{1,0:T(1,128)S(1)} copy-done((f32[1,256]{1,0:T(1,128)S(1)}, f32[1,256]{1,0:T(1,128)}, u32[]{:S(2)}) %copy-start.6) | copy-done | bytes 1048
  25.6 0.7 %copy-done.7 = s32[1,256]{1,0:T(1,128)S(1)} copy-done((s32[1,256]{1,0:T(1,128)S(1)}, s32[1,256]{1,0:T(1,128)}, u32[]{:S(2)}) %copy-start.7) | copy-done | bytes 1048
  26.3 0.7 %copy-done.9 = f32[56]{0:T(128)S(1)} copy-done((f32[56]{0:T(128)S(1)}, f32[56]{0:T(128)}, u32[]{:S(2)}) %copy-start.9) | copy-done | bytes 248
  26.9 0.7 %copy-done.10 = f32[56]{0:T(128)S(1)} copy-done((f32[56]{0:T(128)S(1)}, f32[56]{0:T(128)}, u32[]{:S(2)}) %copy-start.10) | copy-done | bytes 248
  27.6 4.3 %radiation.1 = (f32[90,256]{1,0:T(8,128)S(1)}, f32[90,1,256]{2,1,0:T(1,128)}, f32[90,1,256]{2,1,0:T(1,128)S(1)}) custom-call(f32[184,256]{1,0:T(8,128)S(1)} %get-tuple-element.18.base, f32[184,256]{1,0:T(8,128)S(1)} %collective-permute-done.2.share, f32[56,256]{1,0:T(8,128)S(1)} %get-tuple-element.20.weights, f32[90,56,128]{2,1,0:T(8,128)S(1)} %get-tuple-element.21.dry, ...), custom_call_target="tpu_custom_call" | custom-call | flops 4194304 | bytes 2097152 | tf_op jit(solution)/shard_map/radiation/pallas_call | solution.py:255
  31.8 0.1 collective-permute-start.3
  32.0 1.2 %collective-permute-done.3 = f32[90,256]{1,0:T(8,128)S(1)} collective-permute-done((f32[90,256]{1,0:T(8,128)S(1)}, f32[90,256]{1,0:T(8,128)S(1)}, u32[]{:S(2)}, u32[]{:S(2)}) %collective-permute-start.3) | collective-permute-done | bytes 92192 | tf_op jit(solution)/shard_map/ppermute | solution.py:242
  33.2 1.6 %collective-permute-start.4 = (f32[90,256]{1,0:T(8,128)S(1)}, f32[90,256]{1,0:T(8,128)S(1)}, u32[]{:S(2)}, u32[]{:S(2)}) collective-permute-start(f32[90,256]{1,0:T(8,128)S(1)} %add.3.one), channel_id=1, source_target_pairs={{0,2},{1,3},{2,0},{3,1},{4,6},{5,7},{6,4},{7,5},{8,10},{9,11},{10,... | collective-permute-start | bytes 276488 | tf_op jit(solution)/shard_map/ppermute | solution.py:242
  34.7 3.4 %collective-permute-done.4.two = f32[90,256]{1,0:T(8,128)S(1)} collective-permute-done((f32[90,256]{1,0:T(8,128)S(1)}, f32[90,256]{1,0:T(8,128)S(1)}, u32[]{:S(2)}, u32[]{:S(2)}) %collective-permute-start.4) | collective-permute-done | bytes 92192 | tf_op jit(solution)/shard_map/ppermute | solution.py:242
  38.1 0.7 %final.1 = (f32[90,1,256]{2,1,0:T(1,128)}, f32[90,1,256]{2,1,0:T(1,128)}) custom-call(f32[90,256]{1,0:T(8,128)S(1)} %add.3.one, f32[90,256]{1,0:T(8,128)S(1)} %collective-permute-done.4.two, f32[90,1,256]{2,1,0:T(1,128)S(1)} %get-tuple-element.23.temp), custom_call_target="tpu_custom_call" | custom-call | flops 4194304 | bytes 2097152 | tf_op jit(solution)/shard_map/final/pallas_call | solution.py:268
  (8 shorter events, 0.0 us)
Async XLA Ops:
  0.6 0.9 %copy-start = (f32[56,512]{1,0:T(8,128)S(1)}, f32[56,512]{1,0:T(8,128)}, u32[]{:S(2)}) copy-start(f32[56,512]{1,0:T(8,128)} %factors.1) | copy-start | bytes 344068
  1.5 0.9 %copy-start.1 = (f32[90,1,256]{2,1,0:T(1,128)S(1)}, f32[90,1,256]{2,1,0:T(1,128)}, u32[]{:S(2)}) copy-start(f32[90,1,256]{2,1,0:T(1,128)} %kelvin.1) | copy-start | bytes 276484
  2.4 0.9 %copy-start.2 = (f32[90,1,256]{2,1,0:T(1,128)S(1)}, f32[90,1,256]{2,1,0:T(1,128)}, u32[]{:S(2)}) copy-start(f32[90,1,256]{2,1,0:T(1,128)} %moisture.1) | copy-start | bytes 276484
  3.3 0.7 %copy-start.4 = (f32[1,256]{1,0:T(1,128)S(1)}, f32[1,256]{1,0:T(1,128)}, u32[]{:S(2)}) copy-start(f32[1,256]{1,0:T(1,128)} %spread.1) | copy-start | bytes 3076
  4.8 15.0 %all-to-all-start = ((f32[8,32,128]{2,1,0:T(8,128)}), f32[8,32,128]{2,1,0:T(8,128)S(1)}, u32[]{:S(2)}, u32[]{:S(2)}) async-start(f32[8,32,128]{2,1,0:T(8,128)} %get-tuple-element.16), calls=%async_computation | async-start | bytes 262144 | tf_op jit(solution)/shard_map/all_to_all | solution.py:223
  12.1 11.0 %collective-permute-start.1 = (f32[184,256]{1,0:T(8,128)S(1)}, f32[184,256]{1,0:T(8,128)S(1)}, u32[]{:S(2)}, u32[]{:S(2)}) collective-permute-start(f32[184,256]{1,0:T(8,128)S(1)} %get-tuple-element.15.fields), channel_id=1, source_target_pairs={{9,1},{11,3},{13,5},{15,7},{0,8},{17,9},{2,10},{19,11},{4,12},{21,... | collective-permute-start | bytes 565256 | tf_op jit(solution)/shard_map/ppermute | solution.py:239
  16.0 7.1 %collective-permute-start = (f32[184,256]{1,0:T(8,128)S(1)}, f32[184,256]{1,0:T(8,128)S(1)}, u32[]{:S(2)}, u32[]{:S(2)}) collective-permute-start(f32[184,256]{1,0:T(8,128)S(1)} %get-tuple-element.15.fields), channel_id=1, source_target_pairs={{5,1},{7,3},{0,4},{9,5},{2,6},{11,7},{4,8},{13,9},{6,10},{15,11},{... | collective-permute-start | bytes 565256 | tf_op jit(solution)/shard_map/ppermute | solution.py:239
  19.7 0.7 %copy-start.3 = (f32[56,90]{1,0:T(8,128)S(1)}, f32[56,90]{1,0:T(8,128)}, u32[]{:S(2)}) copy-start(f32[56,90]{1,0:T(8,128)} %arid.1) | copy-start | bytes 60484
  20.5 0.7 %copy-start.5 = (s32[256,1]{0,1:T(1,128)S(1)}, s32[256,1]{0,1:T(1,128)}, u32[]{:S(2)}) copy-start(s32[256,1]{0,1:T(1,128)} %param.16) | copy-start | bytes 3076
  21.2 0.7 %copy-start.8 = (f32[56]{0:T(128)S(1)}, f32[56]{0:T(128)}, u32[]{:S(2)}) copy-start(f32[56]{0:T(128)} %param.19) | copy-start | bytes 676
  23.4 1.5 %collective-permute-start.2 = (f32[184,256]{1,0:T(8,128)S(1)}, f32[184,256]{1,0:T(8,128)S(1)}, u32[]{:S(2)}, u32[]{:S(2)}) collective-permute-start(f32[184,256]{1,0:T(8,128)S(1)} %get-tuple-element.19), channel_id=1, source_target_pairs={{0,1},{1,0},{2,3},{3,2},{4,5},{5,4},{6,7},{7,6},{8,9},{9,8},{10,11... | collective-permute-start | bytes 565256 | tf_op jit(solution)/shard_map/ppermute | solution.py:242
  24.9 0.7 %copy-start.6 = (f32[1,256]{1,0:T(1,128)S(1)}, f32[1,256]{1,0:T(1,128)}, u32[]{:S(2)}) copy-start(f32[1,256]{1,0:T(1,128)} %angle.1) | copy-start | bytes 3076
  25.6 0.7 %copy-start.7 = (s32[1,256]{1,0:T(1,128)S(1)}, s32[1,256]{1,0:T(1,128)}, u32[]{:S(2)}) copy-start(s32[1,256]{1,0:T(1,128)} %lit.1) | copy-start | bytes 3076
  26.3 0.7 %copy-start.9 = (f32[56]{0:T(128)S(1)}, f32[56]{0:T(128)}, u32[]{:S(2)}) copy-start(f32[56]{0:T(128)} %param.20) | copy-start | bytes 676
  26.9 0.7 %copy-start.10 = (f32[56]{0:T(128)S(1)}, f32[56]{0:T(128)}, u32[]{:S(2)}) copy-start(f32[56]{0:T(128)} %param.21) | copy-start | bytes 676
  31.8 1.3 %collective-permute-start.3 = (f32[90,256]{1,0:T(8,128)S(1)}, f32[90,256]{1,0:T(8,128)S(1)}, u32[]{:S(2)}, u32[]{:S(2)}) collective-permute-start(f32[90,256]{1,0:T(8,128)S(1)} %get-tuple-element.22), channel_id=1, source_target_pairs={{0,1},{1,0},{2,3},{3,2},{4,5},{5,4},{6,7},{7,6},{8,9},{9,8},{10,11... | collective-permute-start | bytes 276488 | tf_op jit(solution)/shard_map/ppermute | solution.py:242
  33.2 4.9 %collective-permute-start.4 = (f32[90,256]{1,0:T(8,128)S(1)}, f32[90,256]{1,0:T(8,128)S(1)}, u32[]{:S(2)}, u32[]{:S(2)}) collective-permute-start(f32[90,256]{1,0:T(8,128)S(1)} %add.3.one), channel_id=1, source_target_pairs={{0,2},{1,3},{2,0},{3,1},{4,6},{5,7},{6,4},{7,5},{8,10},{9,11},{10,... | collective-permute-start | bytes 276488 | tf_op jit(solution)/shard_map/ppermute | solution.py:242

commit v2 on v1

--- a/solution.py
+++ b/solution.py
@@ -10,17 +10,19 @@
 
 LOG2E = math.log2(math.e)
 VM = pl.BlockSpec(memory_space=pltpu.VMEM)
-
-
-def kernel_call(body, out_shapes, scratch=(), flops=1 << 22, name=None):
+FAR = pl.BlockSpec(memory_space=pltpu.HBM)
+
+
+def kernel_call(body, outs, scratch=(), in_specs=None, flops=1 << 22, name=None):
     return pl.pallas_call(
         body,
-        out_shape=[jax.ShapeDtypeStruct(s, jnp.float32) for s in out_shapes],
-        out_specs=[VM] * len(out_shapes),
+        out_shape=[o if hasattr(o, "dtype") else jax.ShapeDtypeStruct(o, jnp.float32) for o in outs],
+        out_specs=[VM] * len(outs),
         scratch_shapes=list(scratch),
         compiler_params=pltpu.CompilerParams(vmem_limit_bytes=24 << 20),
         cost_estimate=pl.CostEstimate(flops=flops, bytes_accessed=1 << 21, transcendentals=0),
         name=name,
+        **({} if in_specs is None else {"in_specs": in_specs}),
     )
 
 
@@ -44,31 +46,39 @@
     return pltpu.roll(v, width - 1, 1) + pltpu.roll(v, 1, 1) - 4.0 * v
 
 
-def pack_kernel(cap, kelvin, moisture, spread, factors, fields, blocks):
+def pack_kernel(cap, packed, kept, *refs):
+    n_in = kept + 3 + packed
+    given, rest = refs[:n_in], refs[n_in:]
+    outs, scratch, sems = rest[: 1 + packed + kept], rest[1 + packed + kept : -1], rest[-1]
+    targets = tuple(scratch) + tuple(outs[1 + packed :])
+    copies = [pltpu.make_async_copy(g, t, sems.at[i]) for i, (g, t) in enumerate(zip(given, targets))]
+    for copy in copies:
+        copy.start()
+    fields = outs[0]
+    if packed:
+        factors, blocks = scratch[0], outs[1]
+        tiles, rows, _ = blocks.shape
+        top = factors.shape[0] - rows
+        lane = lax.broadcasted_iota(jnp.int32, (rows, 2 * cap), 1)
+        copies[0].wait()
+        for pair in range(tiles // 2):
+            first = factors[0:rows, pair * 2 * cap : (pair + 1) * 2 * cap]
+            second = factors[top : top + rows, pair * 2 * cap : (pair + 1) * 2 * cap]
+            blocks[2 * pair] = jnp.where(lane < cap, first, pltpu.roll(second, cap, 1))
+            blocks[2 * pair + 1] = jnp.where(lane < cap, pltpu.roll(first, cap, 1), second)
+    kelvin, moisture, spread = scratch[packed:]
+    for copy in copies[packed : packed + 3]:
+        copy.wait()
     levels = kelvin.shape[0]
-    tiles, rows, _ = blocks.shape
-    top = factors.shape[0] - rows
-    lane = lax.broadcasted_iota(jnp.int32, (rows, 2 * cap), 1)
-    for pair in range(tiles // 2):
-        first = factors[0:rows, pair * 2 * cap : (pair + 1) * 2 * cap]
-        second = factors[top : top + rows, pair * 2 * cap : (pair + 1) * 2 * cap]
-        blocks[2 * pair] = jnp.where(lane < cap, first, pltpu.roll(second, cap, 1))
-        blocks[2 * pair + 1] = jnp.where(lane < cap, pltpu.roll(first, cap, 1), second)
-    stack_fields(levels, kelvin, moisture, spread, fields)
-
-
-def stack_fields(levels, kelvin, moisture, spread, fields):
     for l in range(levels):
         fields[l : l + 1, :] = kelvin[l]
         fields[levels + l : levels + l + 1, :] = moisture[l]
     fields[2 * levels : 2 * levels + 1, :] = spread[...]
-    rest = fields.shape[0] - 2 * levels - 1
-    if rest:
-        fields[2 * levels + 1 :, :] = jnp.zeros((rest, fields.shape[1]), jnp.float32)
-
-
-def fields_kernel(kelvin, moisture, spread, fields):
-    stack_fields(kelvin.shape[0], kelvin, moisture, spread, fields)
+    left = fields.shape[0] - 2 * levels - 1
+    if left:
+        fields[2 * levels + 1 :, :] = jnp.zeros((left, fields.shape[1]), jnp.float32)
+    for copy in copies[packed + 3 :]:
+        copy.wait()
 
 
 def gather_kernel(cap, tiles, packed, levels, homed, owners, vapour, arid, fields, weights, dry, base):
@@ -215,16 +225,26 @@
         raise ValueError("unsupported shapes")
     stacked = -(-(2 * levels + 1) // 8) * 8
     packed = 2 * cap == 128 and gpoints % 16 == 8 and n_tile % 2 == 0
+    half = (gpoints + 8) // 2
+    inputs = [factors] * packed + [kelvin, moisture, spreading_number]
+    row = (1, gpoints)
+    small = [owners.reshape(1, width), vapour_absorption.reshape(row), arid]
+    small += [angle, lit, black.reshape(row), solar.reshape(row)]
+    outs = [jax.ShapeDtypeStruct((stacked, width), jnp.float32)]
+    outs += [jax.ShapeDtypeStruct((n_tile, half, 128), jnp.float32)] * packed
+    results = kernel_call(
+        functools.partial(pack_kernel, cap, packed, len(small)),
+        outs + [jax.ShapeDtypeStruct(v.shape, v.dtype) for v in small],
+        scratch=[pltpu.VMEM(v.shape, v.dtype) for v in inputs]
+        + [pltpu.SemaphoreType.DMA((len(inputs) + len(small),))],
+        in_specs=[FAR] * (len(inputs) + len(small)),
+        name="pack",
+    )(*(pltpu.with_memory_space_constraint(v, pltpu.HBM) for v in inputs + small))
+    fields = results[0]
+    owners, vapour_absorption, arid, angle, lit, black, solar = results[1 + packed :]
     if packed:
-        half = (gpoints + 8) // 2
-        fields, blocks = kernel_call(
-            functools.partial(pack_kernel, cap), [(stacked, width), (n_tile, half, 128)], name="pack"
-        )(kelvin, moisture, spreading_number, factors)
-        homed = lax.all_to_all(blocks, "tile", split_axis=0, concat_axis=0, tiled=True)
+        homed = lax.all_to_all(results[1], "tile", split_axis=0, concat_axis=0, tiled=True)
     else:
-        (fields,) = kernel_call(fields_kernel, [(stacked, width)], name="pack")(
-            kelvin, moisture, spreading_number
-        )
         blocks = factors.reshape(gpoints, n_tile, cap)
         homed = lax.all_to_all(blocks, "tile", split_axis=1, concat_axis=1, tiled=True)
         homed = homed.reshape(gpoints, slots)
@@ -247,7 +267,7 @@
         functools.partial(gather_kernel, cap, n_tile, packed, levels),
         [(gpoints, width), (levels, gpoints, 128), (stacked, width)],
         name="gather",
-    )(homed, owners.reshape(1, width), vapour_absorption.reshape(1, gpoints), arid, fields)
+    )(homed, owners, vapour_absorption, arid, fields)
     share, mine = kernel_call(
         functools.partial(side_kernel, levels), [(stacked, width)] * 2, name="side"
     )(fields, near, far, base)
@@ -260,7 +280,7 @@
             pltpu.VMEM((width // 128, levels * 8, 128), jnp.float32),
         ],
         name="radiation",
-    )(mine, other, weights, dry, angle, lit, black.reshape(1, gpoints), solar.reshape(1, gpoints))
+    )(mine, other, weights, dry, angle, lit, black, solar)
     bit = 1
     while 2 * bit < n_grp:
         part = part + swapped(part, bit)

time: 39.3 us -> 33.9 us (0.86)
  local copies, waits for them, and re-layouts: 8.1 us -> 0 us
  waiting for transfers between devices: 6.31 us -> 7.78 us
  Pallas kernels: 7.3 us -> 8.37 us
    unnamed x22 -> x0, local copies, waits for them, and re-layouts: 8.1 us -> none
    ppermute x2, waiting for transfers between devices: 0.01 us -> 1.47 us  [from_side(): return lax.ppermute(fields, ('tile', 'grp'), pairs)]
    pallas_call x1, Pallas kernels: 0.76 us -> 1.84 us  [on_device(): kernel_call(functools.partial(pack_kernel, cap, packed, len(small)), outs...]
  transfers between devices with their start and end apart: 6 -> 6, of which waited for: 4 -> 5; matrix products, arithmetic and copies ran while one was open for 0% -> 0% of each run, Pallas kernels for 3% -> 4%
where the time goes in v2:
time: 33.9 us; the launch traced here: 33.3 us
  starting transfers between devices  16.4 us (48%)
  Pallas kernels  8.37 us (25%)
  waiting for transfers between devices  7.78 us (23%)
  between operations  0.7 us (2%)
    all_to_all x1, starting transfers between devices, on_device(): lax.all_to_all(results[1], 'tile', split_axis=0, concat_axis=0, tiled=True)  7.32 us
    ppermute x2, starting transfers between devices, from_side(): return lax.ppermute(fields, ('tile', 'grp'), pairs)  7.3 us
    ppermute x3, waiting for transfers between devices, swapped(): return lax.ppermute(x, 'grp', [(i, i ^ bit) for i in range(n_grp)])  5.94 us
    pallas_call x1, Pallas kernels, on_device(): kernel_call(functools.partial(radiation_kernel, levels, gpoints), [(level...  4.27 us
    pallas_call x1, Pallas kernels, on_device(): kernel_call(functools.partial(pack_kernel, cap, packed, len(small)), outs...  1.84 us
    ppermute x3, starting transfers between devices, swapped(): return lax.ppermute(x, 'grp', [(i, i ^ bit) for i in range(n_grp)])  1.77 us
    ppermute x2, waiting for transfers between devices, from_side(): return lax.ppermute(fields, ('tile', 'grp'), pairs)  1.47 us
    pallas_call x1, Pallas kernels, on_device(): kernel_call(functools.partial(gather_kernel, cap, n_tile, packed, levels)...  1.22 us
  transfers between devices with their start and end apart: 6, of which 5 were waited for; matrix products, arithmetic and copies ran while one was open for 0% of the time, Pallas kernels for 4%

profile of v2, /device:TPU:0, one launch (start us, length us, event | category | flops | bytes accessed | tf_op | source)
XLA Modules:
  0.0 33.3 jit_solution(7204594152006988199)
XLA Ops:
  0.6 1.8 %pack.1 = (f32[184,256]{1,0:T(8,128)S(1)}, f32[8,32,128]{2,1,0:T(8,128)}, s32[1,256]{1,0:T(1,128)S(1)}, f32[1,56]{1,0:T(1,128)S(1)}, f32[56,90]{1,0:T(8,128)S(1)...) custom-call(f32[56,512]{1,0:T(8,128)} %refs_0_.1, ...), custom_call_target="tpu_custom_call" | custom-call | flops 4194304 | bytes 2097152 | tf_op jit(solution)/shard_map/pack/pallas_call | solution.py:235
  2.5 7.3 %all-to-all-start = ((f32[8,32,128]{2,1,0:T(8,128)}), f32[8,32,128]{2,1,0:T(8,128)S(1)}, u32[]{:S(2)}, u32[]{:S(2)}) async-start(f32[8,32,128]{2,1,0:T(8,128)} %get-tuple-element.23), calls=%async_computation | async-start | bytes 262144 | tf_op jit(solution)/shard_map/all_to_all | solution.py:246
  9.8 3.9 %collective-permute-start.1 = (f32[184,256]{1,0:T(8,128)S(1)}, f32[184,256]{1,0:T(8,128)S(1)}, u32[]{:S(2)}, u32[]{:S(2)}) collective-permute-start(f32[184,256]{1,0:T(8,128)S(1)} %get-tuple-element.22.fields), channel_id=1, source_target_pairs={{9,1},{11,3},{13,5},{15,7},{0,8},{17,9},{2,10},{19,11},{4,12},{21,... | collective-permute-start | bytes 565256 | tf_op jit(solution)/shard_map/ppermute | solution.py:259
  13.7 3.4 %collective-permute-start = (f32[184,256]{1,0:T(8,128)S(1)}, f32[184,256]{1,0:T(8,128)S(1)}, u32[]{:S(2)}, u32[]{:S(2)}) collective-permute-start(f32[184,256]{1,0:T(8,128)S(1)} %get-tuple-element.22.fields), channel_id=1, source_target_pairs={{5,1},{7,3},{0,4},{9,5},{2,6},{11,7},{4,8},{13,9},{6,10},{15,11},{... | collective-permute-start | bytes 565256 | tf_op jit(solution)/shard_map/ppermute | solution.py:259
  17.1 0.4 %all-to-all-done.homed = f32[8,32,128]{2,1,0:T(8,128)S(1)} async-done(((f32[8,32,128]{2,1,0:T(8,128)}), f32[8,32,128]{2,1,0:T(8,128)S(1)}, u32[]{:S(2)}, u32[]{:S(2)}) %all-to-all-start) | async-done | bytes 131104 | tf_op jit(solution)/shard_map/all_to_all | solution.py:246
  17.5 1.2 %gather.1 = (f32[56,256]{1,0:T(8,128)S(1)}, f32[90,56,128]{2,1,0:T(8,128)S(1)}, f32[184,256]{1,0:T(8,128)S(1)}) custom-call(f32[8,32,128]{2,1,0:T(8,128)S(1)} %all-to-all-done.homed, s32[1,256]{1,0:T(1,128)S(1)} %get-tuple-element.24.owners, f32[1,56]{1,0:T(1,128)S(1)} %get-tuple-element.25.vapour, f32[56,90]{1,0:T(8,128)S(1)} %get-tuple-element.26.arid, ...), custom_call_target="tpu_custom_call" | custom-call | flops 4194304 | bytes 2097152 | tf_op jit(solution)/shard_map/gather/pallas_call | solution.py:266
  18.7 0.0 collective-permute-done.1.far
  18.7 1.5 %collective-permute-done.near = f32[184,256]{1,0:T(8,128)S(1)} collective-permute-done((f32[184,256]{1,0:T(8,128)S(1)}, f32[184,256]{1,0:T(8,128)S(1)}, u32[]{:S(2)}, u32[]{:S(2)}) %collective-permute-start) | collective-permute-done | bytes 188448 | tf_op jit(solution)/shard_map/ppermute | solution.py:259
  20.2 0.3 side.1
  20.5 0.1 collective-permute-start.2
  20.6 1.4 %collective-permute-done.2.share = f32[184,256]{1,0:T(8,128)S(1)} collective-permute-done((f32[184,256]{1,0:T(8,128)S(1)}, f32[184,256]{1,0:T(8,128)S(1)}, u32[]{:S(2)}, u32[]{:S(2)}) %collective-permute-start.2) | collective-permute-done | bytes 188448 | tf_op jit(solution)/shard_map/ppermute | solution.py:262
  22.0 4.3 %radiation.1 = (f32[90,256]{1,0:T(8,128)S(1)}, f32[90,1,256]{2,1,0:T(1,128)}, f32[90,1,256]{2,1,0:T(1,128)S(1)}) custom-call(f32[184,256]{1,0:T(8,128)S(1)} %get-tuple-element.28.base, f32[184,256]{1,0:T(8,128)S(1)} %collective-permute-done.2.share, f32[56,256]{1,0:T(8,128)S(1)} %get-tuple-element.30.weights, f32[90,56,128]{2,1,0:T(8,128)S(1)} %get-tuple-element.31.dry, ...), custom_call_target="tpu_custom_call" | custom-call | flops 4194304 | bytes 2097152 | tf_op jit(solution)/shard_map/radiation/pallas_call | solution.py:275
  26.3 0.1 collective-permute-start.3
  26.4 1.2 %collective-permute-done.3 = f32[90,256]{1,0:T(8,128)S(1)} collective-permute-done((f32[90,256]{1,0:T(8,128)S(1)}, f32[90,256]{1,0:T(8,128)S(1)}, u32[]{:S(2)}, u32[]{:S(2)}) %collective-permute-start.3) | collective-permute-done | bytes 92192 | tf_op jit(solution)/shard_map/ppermute | solution.py:262
  27.6 1.6 %collective-permute-start.4 = (f32[90,256]{1,0:T(8,128)S(1)}, f32[90,256]{1,0:T(8,128)S(1)}, u32[]{:S(2)}, u32[]{:S(2)}) collective-permute-start(f32[90,256]{1,0:T(8,128)S(1)} %add.3.one), channel_id=1, source_target_pairs={{0,2},{1,3},{2,0},{3,1},{4,6},{5,7},{6,4},{7,5},{8,10},{9,11},{10,... | collective-permute-start | bytes 276488 | tf_op jit(solution)/shard_map/ppermute | solution.py:262
  29.2 3.4 %collective-permute-done.4.two = f32[90,256]{1,0:T(8,128)S(1)} collective-permute-done((f32[90,256]{1,0:T(8,128)S(1)}, f32[90,256]{1,0:T(8,128)S(1)}, u32[]{:S(2)}, u32[]{:S(2)}) %collective-permute-start.4) | collective-permute-done | bytes 92192 | tf_op jit(solution)/shard_map/ppermute | solution.py:262
  32.5 0.7 %final.1 = (f32[90,1,256]{2,1,0:T(1,128)}, f32[90,1,256]{2,1,0:T(1,128)}) custom-call(f32[90,256]{1,0:T(8,128)S(1)} %add.3.one, f32[90,256]{1,0:T(8,128)S(1)} %collective-permute-done.4.two, f32[90,1,256]{2,1,0:T(1,128)S(1)} %get-tuple-element.37.temp), custom_call_target="tpu_custom_call" | custom-call | flops 4194304 | bytes 2097152 | tf_op jit(solution)/shard_map/final/pallas_call | solution.py:288
  (1 shorter events, 0.0 us)
Async XLA Ops:
  2.5 15.0 %all-to-all-start = ((f32[8,32,128]{2,1,0:T(8,128)}), f32[8,32,128]{2,1,0:T(8,128)S(1)}, u32[]{:S(2)}, u32[]{:S(2)}) async-start(f32[8,32,128]{2,1,0:T(8,128)} %get-tuple-element.23), calls=%async_computation | async-start | bytes 262144 | tf_op jit(solution)/shard_map/all_to_all | solution.py:246
  9.8 8.9 %collective-permute-start.1 = (f32[184,256]{1,0:T(8,128)S(1)}, f32[184,256]{1,0:T(8,128)S(1)}, u32[]{:S(2)}, u32[]{:S(2)}) collective-permute-start(f32[184,256]{1,0:T(8,128)S(1)} %get-tuple-element.22.fields), channel_id=1, source_target_pairs={{9,1},{11,3},{13,5},{15,7},{0,8},{17,9},{2,10},{19,11},{4,12},{21,... | collective-permute-start | bytes 565256 | tf_op jit(solution)/shard_map/ppermute | solution.py:259
  13.7 6.5 %collective-permute-start = (f32[184,256]{1,0:T(8,128)S(1)}, f32[184,256]{1,0:T(8,128)S(1)}, u32[]{:S(2)}, u32[]{:S(2)}) collective-permute-start(f32[184,256]{1,0:T(8,128)S(1)} %get-tuple-element.22.fields), channel_id=1, source_target_pairs={{5,1},{7,3},{0,4},{9,5},{2,6},{11,7},{4,8},{13,9},{6,10},{15,11},{... | collective-permute-start | bytes 565256 | tf_op jit(solution)/shard_map/ppermute | solution.py:259
  20.5 1.5 %collective-permute-start.2 = (f32[184,256]{1,0:T(8,128)S(1)}, f32[184,256]{1,0:T(8,128)S(1)}, u32[]{:S(2)}, u32[]{:S(2)}) collective-permute-start(f32[184,256]{1,0:T(8,128)S(1)} %get-tuple-element.29), channel_id=1, source_target_pairs={{0,1},{1,0},{2,3},{3,2},{4,5},{5,4},{6,7},{7,6},{8,9},{9,8},{10,11... | collective-permute-start | bytes 565256 | tf_op jit(solution)/shard_map/ppermute | solution.py:262
  26.3 1.3 %collective-permute-start.3 = (f32[90,256]{1,0:T(8,128)S(1)}, f32[90,256]{1,0:T(8,128)S(1)}, u32[]{:S(2)}, u32[]{:S(2)}) collective-permute-start(f32[90,256]{1,0:T(8,128)S(1)} %get-tuple-element.36), channel_id=1, source_target_pairs={{0,1},{1,0},{2,3},{3,2},{4,5},{5,4},{6,7},{7,6},{8,9},{9,8},{10,11... | collective-permute-start | bytes 276488 | tf_op jit(solution)/shard_map/ppermute | solution.py:262
  27.6 4.9 %collective-permute-start.4 = (f32[90,256]{1,0:T(8,128)S(1)}, f32[90,256]{1,0:T(8,128)S(1)}, u32[]{:S(2)}, u32[]{:S(2)}) collective-permute-start(f32[90,256]{1,0:T(8,128)S(1)} %add.3.one), channel_id=1, source_target_pairs={{0,2},{1,3},{2,0},{3,1},{4,6},{5,7},{6,4},{7,5},{8,10},{9,11},{10,... | collective-permute-start | bytes 276488 | tf_op jit(solution)/shard_map/ppermute | solution.py:262

commit v3 on v2

v3 whole, which is shorter than its diff:
```python
import functools
import math

import jax
import jax.numpy as jnp
from jax import lax
from jax.experimental import pallas as pl
from jax.experimental.pallas import tpu as pltpu
from jax.sharding import PartitionSpec as P


LOG2E = math.log2(math.e)
VM = pl.BlockSpec(memory_space=pltpu.VMEM)
FAR = pl.BlockSpec(memory_space=pltpu.HBM)


def kernel_call(body, outs, scratch=(), in_specs=None, out_specs=None, flops=1 << 22):
    return pl.pallas_call(
        body,
        out_shape=[o if hasattr(o, "dtype") else jax.ShapeDtypeStruct(o, jnp.float32) for o in outs],
        out_specs=out_specs or [VM] * len(outs),
        scratch_shapes=list(scratch),
        compiler_params=pltpu.CompilerParams(vmem_limit_bytes=24 << 20),
        cost_estimate=pl.CostEstimate(flops=flops, bytes_accessed=1 << 21, transcendentals=0),
        **({} if in_specs is None else {"in_specs": in_specs}),
    )


def split3(x):
    high = x.astype(jnp.bfloat16)
    rest = x - high.astype(jnp.float32)
    middle = rest.astype(jnp.bfloat16)
    low = (rest - middle.astype(jnp.float32)).astype(jnp.bfloat16)
    return high, middle, low


def column_of(row):
    n = row.shape[1]
    r = lax.broadcasted_iota(jnp.int32, (n, n), 0)
    c = lax.broadcasted_iota(jnp.int32, (n, n), 1)
    return jnp.sum(jnp.where(r == c, jnp.broadcast_to(row, (n, n)), 0.0), axis=1, keepdims=True)


def around(v):
    width = v.shape[1]
    return pltpu.roll(v, width - 1, 1) + pltpu.roll(v, 1, 1) - 4.0 * v


def pack_kernel(cap, packed, kept, *refs):
    n_in = kept + 3 + packed
    given, rest = refs[:n_in], refs[n_in:]
    outs, scratch, sems = rest[: 1 + packed + kept], rest[1 + packed + kept : -1], rest[-1]
    targets = tuple(scratch) + tuple(outs[1 + packed :])
    copies = [pltpu.make_async_copy(g, t, sems.at[i]) for i, (g, t) in enumerate(zip(given, targets))]
    for copy in copies:
        copy.start()
    fields = outs[0]
    if packed:
        factors, blocks = scratch[0], outs[1]
        tiles, rows, _ = blocks.shape
        top = factors.shape[0] - rows
        lane = lax.broadcasted_iota(jnp.int32, (rows, 2 * cap), 1)
        copies[0].wait()
        for pair in range(tiles // 2):
            first = factors[0:rows, pair * 2 * cap : (pair + 1) * 2 * cap]
            second = factors[top : top + rows, pair * 2 * cap : (pair + 1) * 2 * cap]
            blocks[2 * pair] = jnp.where(lane < cap, first, pltpu.roll(second, cap, 1))
            blocks[2 * pair + 1] = jnp.where(lane < cap, pltpu.roll(first, cap, 1), second)
    kelvin, moisture, spread = scratch[packed:]
    for copy in copies[packed : packed + 3]:
        copy.wait()
    levels = kelvin.shape[0]
    for l in range(levels):
        fields[l : l + 1, :] = kelvin[l]
        fields[levels + l : levels + l + 1, :] = moisture[l]
    fields[2 * levels : 2 * levels + 1, :] = spread[...]
    left = fields.shape[0] - 2 * levels - 1
    if left:
        fields[2 * levels + 1 :, :] = jnp.zeros((left, fields.shape[1]), jnp.float32)
    for copy in copies[packed + 3 :]:
        copy.wait()


def prepare_kernel(cap, tiles, levels, owners, fields, choice, base):
    columns = owners.shape[1]
    owner = owners[...]
    matches = lax.broadcasted_iota(jnp.int32, (tiles, columns), 0) == owner
    member = matches.astype(jnp.float32)
    r = lax.broadcasted_iota(jnp.int32, (columns, columns), 0)
    c = lax.broadcasted_iota(jnp.int32, (columns, columns), 1)
    earlier = (r < c).astype(jnp.float32).astype(jnp.bfloat16)
    counts = jnp.dot(member.astype(jnp.bfloat16), earlier, preferred_element_type=jnp.float32)
    rank = jnp.sum(jnp.where(matches, counts, 0.0), axis=0, keepdims=True)
    slot = owner * cap + rank.astype(jnp.int32)
    chosen = (lax.broadcasted_iota(jnp.int32, (tiles * cap, columns), 0) == slot).astype(jnp.float32)
    choice[...] = chosen.astype(jnp.bfloat16)
    f = fields[...]
    spread = fields[2 * levels : 2 * levels + 1, :]
    f = f + spread * around(f)
    base[...] = f + spread * around(f)


def select_kernel(cap, tiles, packed, levels, homed, choice, vapour, arid, weights, dry):
    gpoints = weights.shape[0]
    if packed:
        rows = homed.shape[1]
        lane = lax.broadcasted_iota(jnp.int32, (rows, 2 * cap), 1)
        lower, upper = [], []
        for pair in range(tiles // 2):
            first, second = homed[2 * pair], homed[2 * pair + 1]
            lower.append(jnp.where(lane < cap, first, pltpu.roll(second, cap, 1)))
            upper.append(jnp.where(lane < cap, pltpu.roll(first, cap, 1), second))
        lower = jnp.concatenate(lower, axis=1)
        upper = jnp.concatenate(upper, axis=1)[2 * rows - gpoints :]
        table = jnp.concatenate([lower, upper], axis=0)
    else:
        table = homed[...]
    picked = 0.0
    for part in split3(table):
        picked = picked + jnp.dot(part, choice[...], preferred_element_type=jnp.float32)
    weights[...] = picked * (column_of(vapour[...]) * -LOG2E)
    for l in range(levels):
        dry[l] = jnp.broadcast_to(arid[:, l : l + 1] * -LOG2E, (gpoints, dry.shape[2]))


def side_kernel(levels, fields, near, far, base, share, total):
    spread = fields[2 * levels : 2 * levels + 1, :]
    near_spread = near[2 * levels : 2 * levels + 1, :]
    f = near[...]
    near_next = f + near_spread * (far[...] + fields[...] + around(f))
    v = spread * f
    part = v + spread * (around(v) + near_next)
    share[...] = part
    total[...] = base[...] + part


def spread_rows(levels, base, share, temp, wet):
    f = base[...] + share[...]
    for l in range(levels):
        temp[l] = f[l : l + 1]
        wet[l] = f[levels + l : levels + l + 1]


def radiation_kernel(
    levels, gpoints, first, temp, wet, weights, dry, angle, lit, black, solar, part, rest, sums
):
    blocks = gpoints // 8
    black_column = jnp.broadcast_to(column_of(black[...]), (gpoints, 128))
    solar_column = jnp.broadcast_to(column_of(solar[...]), (gpoints, 128))
    unroll = max(u for u in range(1, 11) if levels % u == 0)
    parity = lax.rem(lax.axis_index("grp"), 2)
    half = 1 - parity if first else parity
    at = pl.ds(pl.multiple_of(half * 128, 128), 128)
    mu = jnp.broadcast_to(angle[:, at], (8, 128))
    inverse = 1.0 / mu
    marker = mu * jnp.broadcast_to(lit[:, at].astype(jnp.float32), (8, 128))
    share_of = [black_column[8 * b : 8 * b + 8] for b in range(blocks)]
    weight = [weights[8 * b : 8 * b + 8, at] for b in range(blocks)]
    beams = tuple(solar_column[8 * b : 8 * b + 8] * marker for b in range(blocks))
    zero = tuple(jnp.zeros((8, 128), jnp.float32) for _ in range(blocks))

    def down_level(l, carry):
        down, beam = carry
        warm = jnp.broadcast_to(temp[l, :, at], (8, 128))
        moist = jnp.broadcast_to(wet[l, :, at], (8, 128))
        new_down, new_beam, acc = [], [], None
        for b in range(blocks):
            tau = dry[l, 8 * b : 8 * b + 8, :] + weight[b] * moist
            lost = 1.0 - jnp.exp2(tau)
            rest[l, 8 * b : 8 * b + 8, :] = lost
            step = lost * (down[b] - share_of[b] * warm)
            after = beam[b] * jnp.exp2(tau * inverse)
            net = step + (beam[b] - after)
            acc = net if acc is None else acc + net
            new_down.append(down[b] - step)
            new_beam.append(after)
        sums[pl.ds(pl.multiple_of(l * 8, 8), 8), :] = acc
        return tuple(new_down), tuple(new_beam)

    def up_level(i, up):
        l = levels - 1 - i
        warm = jnp.broadcast_to(temp[l, :, at], (8, 128))
        new_up, acc = [], None
        for b in range(blocks):
            step = rest[l, 8 * b : 8 * b + 8, :] * (share_of[b] * warm - up[b])
            acc = step if acc is None else acc + step
            new_up.append(up[b] + step)
        where = pl.ds(pl.multiple_of(l * 8, 8), 8)
        sums[where, :] = sums[where, :] - acc
        return tuple(new_up)

    lax.fori_loop(0, levels, down_level, (zero, beams), unroll=unroll)
    floor = jnp.broadcast_to(temp[levels - 1, :, at], (8, 128))
    lax.fori_loop(0, levels, up_level, tuple(s * floor for s in share_of), unroll=unroll)
    total = sums[pl.ds(0, levels, stride=8), :]
    for s in range(1, 8):
        total = total + sums[pl.ds(s, levels, stride=8), :]
    part[...] = total


def first_half_kernel(
    levels, gpoints, base, share, weights, dry, angle, lit, black, solar, part, temp, wet, *scratch
):
    spread_rows(levels, base, share, temp, wet)
    radiation_kernel(levels, gpoints, True, temp, wet, weights, dry, angle, lit, black, solar, part, *scratch)


def second_half_kernel(
    levels, gpoints, temp, wet, weights, dry, angle, lit, black, solar, part, vapour, rest, sums, sem
):
    copy = pltpu.make_async_copy(wet, vapour, sem)
    copy.start()
    radiation_kernel(
        levels, gpoints, False, temp, wet, weights, dry, angle, lit, black, solar, part, rest, sums
    )
    copy.wait()


def final_kernel(scale, mine, other, temp, heating, temp_next):
    levels = mine.shape[0]
    even = lax.rem(lax.axis_index("grp"), 2) == 0
    own, far = mine[...] * scale, other[...] * scale
    left, right = jnp.where(even, own, far), jnp.where(even, far, own)
    for at, heat in ((slice(0, 128), left), (slice(128, 256), right)):
        for l in range(levels):
            heating[l, :, at] = heat[l : l + 1]
            temp_next[l, :, at] = temp[l, :, at] + heat[l : l + 1]


def on_device(
    n_tile,
    n_grp,
    kelvin,
    moisture,
    spreading_number,
    angle,
    lit,
    owners,
    factors,
    arid,
    vapour_absorption,
    black,
    solar,
):
    levels, rows, width = kelvin.shape
    gpoints, slots = factors.shape
    cap = slots // n_tile
    total_g = gpoints * n_grp
    if rows != 1 or n_grp & (n_grp - 1) or n_grp < 2 or gpoints % 8 or width != 256:
        raise ValueError("unsupported shapes")
    stacked = -(-(2 * levels + 1) // 8) * 8
    packed = 2 * cap == 128 and gpoints % 16 == 8 and n_tile % 2 == 0
    half = (gpoints + 8) // 2
    inputs = [factors] * packed + [kelvin, moisture, spreading_number]
    row = (1, gpoints)
    small = [owners.reshape(1, width), vapour_absorption.reshape(row), arid]
    small += [angle, lit, black.reshape(row), solar.reshape(row)]
    outs = [jax.ShapeDtypeStruct((stacked, width), jnp.float32)]
    outs += [jax.ShapeDtypeStruct((n_tile, half, 128), jnp.float32)] * packed
    results = kernel_call(
        functools.partial(pack_kernel, cap, packed, len(small)),
        outs + [jax.ShapeDtypeStruct(v.shape, v.dtype) for v in small],
        scratch=[pltpu.VMEM(v.shape, v.dtype) for v in inputs]
        + [pltpu.SemaphoreType.DMA((len(inputs) + len(small),))],
        in_specs=[FAR] * (len(inputs) + len(small)),
    )(*(pltpu.with_memory_space_constraint(v, pltpu.HBM) for v in inputs + small))
    fields = results[0]
    owners, vapour_absorption, arid, angle, lit, black, solar = results[1 + packed :]
    if packed:
        homed = lax.all_to_all(results[1], "tile", split_axis=0, concat_axis=0, tiled=True)
    else:
        blocks = factors.reshape(gpoints, n_tile, cap)
        homed = lax.all_to_all(blocks, "tile", split_axis=1, concat_axis=1, tiled=True)
        homed = homed.reshape(gpoints, slots)

    def from_side(distance):
        pairs = []
        for t in range(n_tile):
            for g in range(n_grp):
                s = t - distance if g % 2 == 0 else t + distance
                if 0 <= s < n_tile:
                    pairs.append((s * n_grp + g, t * n_grp + g))
        return lax.ppermute(fields, ("tile", "grp"), pairs)

    def swapped(x, bit):
        return lax.ppermute(x, "grp", [(i, i ^ bit) for i in range(n_grp)])

    near = from_side(1)
    far = from_side(2)
    choice, base = kernel_call(
        functools.partial(prepare_kernel, cap, n_tile, levels),
        [jax.ShapeDtypeStruct((slots, width), jnp.bfloat16), (stacked, width)],
    )(owners, fields)
    weights, dry = kernel_call(
        functools.partial(select_kernel, cap, n_tile, packed, levels),
        [(gpoints, width), (levels, gpoints, 128)],
    )(homed, choice, vapour_absorption, arid)
    share, mine = kernel_call(
        functools.partial(side_kernel, levels), [(stacked, width)] * 2
    )(fields, near, far, base)
    other = swapped(share, 1)
    tables = (weights, dry, angle, lit, black, solar)
    work = [
        pltpu.VMEM((levels, gpoints, 128), jnp.float32),
        pltpu.VMEM((levels * 8, 128), jnp.float32),
    ]
    given, temp, wet = kernel_call(
        functools.partial(first_half_kernel, levels, gpoints),
        [(levels, 128), (levels, 1, width), (levels, 1, width)],
        scratch=work,
    )(mine, other, *tables)
    taken = swapped(given, 1)
    part, vapour_next = kernel_call(
        functools.partial(second_half_kernel, levels, gpoints),
        [(levels, 128), (levels, 1, width)],
        scratch=work + [pltpu.SemaphoreType.DMA],
        out_specs=[VM, FAR],
    )(temp, wet, *tables)
    part = part + taken
    bit = 2
    while bit < n_grp:
        part = part + swapped(part, bit)
        bit *= 2
    heating, temp_next = kernel_call(
        functools.partial(final_kernel, 1.0 / total_g), [(levels, 1, width)] * 2
    )(part, swapped(part, 1), temp)
    return heating, temp_next, vapour_next


def solution(mesh):
    in_specs = (
        P(None, "tile", None),
        P(None, "tile", None),
        P("tile", None),
        P("tile", None),
        P("tile", None),
        P("tile", None),
        P("grp", "tile"),
        P("grp", None),
        P("grp"),
        P("grp"),
        P("grp"),
    )
    out_specs = (P(None, "tile", None), P(None, "tile", None), P(None, "tile", None))

    def body(*args):
        return on_device(mesh.shape["tile"], mesh.shape["grp"], *args)

    return jax.shard_map(body, mesh=mesh, in_specs=in_specs, out_specs=out_specs, check_vma=False)
```

time: 33.9 us -> 33.7 us (level)
  waiting for transfers between devices: 7.78 us -> 10.4 us
  starting transfers between devices: 16.4 us -> 14 us
    all_to_all x1, waiting for transfers between devices: 0.37 us -> 6.51 us  [on_device(): lax.all_to_all(results[1], 'tile', split_axis=0, concat_axis=0, tiled=True)]
    all_to_all x1, starting transfers between devices: 7.32 us -> 3.86 us  [on_device(): lax.all_to_all(results[1], 'tile', split_axis=0, concat_axis=0, tiled=True)]
    ppermute x3 -> x4, waiting for transfers between devices: 5.94 us -> 3.87 us  [swapped(): return lax.ppermute(x, 'grp', [(i, i ^ bit) for i in range(n_grp)])]
    ppermute x2, waiting for transfers between devices: 1.47 us -> 0.01 us  [from_side(): return lax.ppermute(fields, ('tile', 'grp'), pairs)]
    ppermute x2, starting transfers between devices: 7.3 us -> 8.4 us  [from_side(): return lax.ppermute(fields, ('tile', 'grp'), pairs)]
    pallas_call x3 -> x5, Pallas kernels: 5.81 us -> 5.57 us  [the longest x1 1.98 us: on_device(): kernel_call(functools.partial(first_half_kernel, levels, gpoints), [(leve...]
    ppermute x3 -> x4, starting transfers between devices: 1.77 us -> 1.76 us  [swapped(): return lax.ppermute(x, 'grp', [(i, i ^ bit) for i in range(n_grp)])]
  transfers between devices with their start and end apart: 6 -> 7, of which waited for: 5 -> 3; matrix products, arithmetic and copies ran while one was open for 0% -> 0% of each run, Pallas kernels for 4% -> 11%
where the time goes in v3:
time: 33.7 us; the launch traced here: 33.4 us
  starting transfers between devices  14 us (42%)
  waiting for transfers between devices  10.4 us (31%)
  Pallas kernels  8.2 us (24%)
  between operations  0.75 us (2%)
    ppermute x2, starting transfers between devices, from_side(): return lax.ppermute(fields, ('tile', 'grp'), pairs)  8.4 us
    all_to_all x1, waiting for transfers between devices, on_device(): lax.all_to_all(results[1], 'tile', split_axis=0, concat_axis=0, tiled=True)  6.51 us
    ppermute x4, waiting for transfers between devices, swapped(): return lax.ppermute(x, 'grp', [(i, i ^ bit) for i in range(n_grp)])  3.87 us
    all_to_all x1, starting transfers between devices, on_device(): lax.all_to_all(results[1], 'tile', split_axis=0, concat_axis=0, tiled=True)  3.86 us
    pallas_call x1, Pallas kernels, on_device(): kernel_call(functools.partial(first_half_kernel, levels, gpoints), [(leve...  1.98 us
    pallas_call x1, Pallas kernels, on_device(): kernel_call(functools.partial(second_half_kernel, levels, gpoints), [(lev...  1.93 us
    pallas_call x1, Pallas kernels, on_device(): kernel_call(functools.partial(pack_kernel, cap, packed, len(small)), outs...  1.85 us
    ppermute x4, starting transfers between devices, swapped(): return lax.ppermute(x, 'grp', [(i, i ^ bit) for i in range(n_grp)])  1.76 us
  transfers between devices with their start and end apart: 7, of which 3 were waited for; matrix products, arithmetic and copies ran while one was open for 0% of the time, Pallas kernels for 11%

profile of v3, /device:TPU:0, one launch (start us, length us, event | category | flops | bytes accessed | tf_op | source)
XLA Modules:
  0.0 33.4 jit_solution(8548794479458249043)
XLA Ops:
  0.6 1.9 %shard_map.130 = (f32[184,256]{1,0:T(8,128)S(1)}, f32[8,32,128]{2,1,0:T(8,128)}, s32[1,256]{1,0:T(1,128)S(1)}, f32[1,56]{1,0:T(1,128)S(1)}, f32[56,90]{1,0:T(8,1...) custom-call(f32[56,512]{1,0:T(8,128)} %refs_0_.1, ...), custom_call_target="tpu_custom_call" | custom-call | flops 4194304 | bytes 2097152 | tf_op jit(solution)/shard_map/pallas_call | solution.py:260
  2.5 5.0 %collective-permute-start.1 = (f32[184,256]{1,0:T(8,128)S(1)}, f32[184,256]{1,0:T(8,128)S(1)}, u32[]{:S(2)}, u32[]{:S(2)}) collective-permute-start(f32[184,256]{1,0:T(8,128)S(1)} %get-tuple-element.25.fields), channel_id=1, source_target_pairs={{9,1},{11,3},{13,5},{15,7},{0,8},{17,9},{2,10},{19,11},{4,12},{21,... | collective-permute-start | bytes 565256 | tf_op jit(solution)/shard_map/ppermute | solution.py:283
  7.5 3.4 %collective-permute-start = (f32[184,256]{1,0:T(8,128)S(1)}, f32[184,256]{1,0:T(8,128)S(1)}, u32[]{:S(2)}, u32[]{:S(2)}) collective-permute-start(f32[184,256]{1,0:T(8,128)S(1)} %get-tuple-element.25.fields), channel_id=1, source_target_pairs={{5,1},{7,3},{0,4},{9,5},{2,6},{11,7},{4,8},{13,9},{6,10},{15,11},{... | collective-permute-start | bytes 565256 | tf_op jit(solution)/shard_map/ppermute | solution.py:283
  10.9 3.9 %all-to-all-start = ((f32[8,32,128]{2,1,0:T(8,128)}), f32[8,32,128]{2,1,0:T(8,128)S(1)}, u32[]{:S(2)}, u32[]{:S(2)}) async-start(f32[8,32,128]{2,1,0:T(8,128)} %get-tuple-element.30), calls=%async_computation | async-start | bytes 262144 | tf_op jit(solution)/shard_map/all_to_all | solution.py:270
  14.8 0.4 %shard_map.131 = (bf16[512,256]{1,0:T(8,128)(2,1)S(1)}, f32[184,256]{1,0:T(8,128)S(1)}) custom-call(s32[1,256]{1,0:T(1,128)S(1)} %get-tuple-element.26.owners, f32[184,256]{1,0:T(8,128)S(1)} %get-tuple-element.25.fields), custom_call_target="tpu_custom_call" | custom-call | flops 4194304 | bytes 2097152 | tf_op jit(solution)/shard_map/pallas_call | solution.py:290
  15.2 0.0 collective-permute-done.1.far
  15.2 0.0 collective-permute-done.near
  15.2 0.3 shard_map.132
  15.5 0.1 collective-permute-start.2
  15.6 6.5 %all-to-all-done.homed = f32[8,32,128]{2,1,0:T(8,128)S(1)} async-done(((f32[8,32,128]{2,1,0:T(8,128)}), f32[8,32,128]{2,1,0:T(8,128)S(1)}, u32[]{:S(2)}, u32[]{:S(2)}) %all-to-all-start) | async-done | bytes 131104 | tf_op jit(solution)/shard_map/all_to_all | solution.py:270
  22.1 0.9 %shard_map.133 = (f32[56,256]{1,0:T(8,128)S(1)}, f32[90,56,128]{2,1,0:T(8,128)S(1)}) custom-call(f32[8,32,128]{2,1,0:T(8,128)S(1)} %all-to-all-done.homed, bf16[512,256]{1,0:T(8,128)(2,1)S(1)} %get-tuple-element.31.choice, f32[1,56]{1,0:T(1,128)S(1)} %get-tuple-element.32.vapour, f32[56,90]{1,0:T(8,128)S(1)} %get-tuple-element.33.arid), custom_call_target="tpu_custom_call" | custom-call | flops 4194304 | bytes 2097152 | tf_op jit(solution)/shard_map/pallas_call | solution.py:294
  23.1 0.0 collective-permute-done.2.share
  23.1 2.0 %shard_map.134 = (f32[90,128]{1,0:T(8,128)S(1)}, f32[90,1,256]{2,1,0:T(1,128)S(1)}, f32[90,1,256]{2,1,0:T(1,128)S(1)}) custom-call(f32[184,256]{1,0:T(8,128)S(1)} %get-tuple-element.28.base, f32[184,256]{1,0:T(8,128)S(1)} %collective-permute-done.2.share, f32[56,256]{1,0:T(8,128)S(1)} %get-tuple-element.34.weights, ...), custom_call_target="tpu_custom_call" | custom-call | flops 4194304 | bytes 2097152 | tf_op jit(solution)/shard_map/pallas_call | solution.py:307
  25.1 0.1 collective-permute-start.3
  25.1 1.9 %shard_map.135 = (f32[90,128]{1,0:T(8,128)S(1)}, f32[90,1,256]{2,1,0:T(1,128)}) custom-call(f32[90,1,256]{2,1,0:T(1,128)S(1)} %get-tuple-element.40.temp, f32[90,1,256]{2,1,0:T(1,128)S(1)} %get-tuple-element.41.wet, f32[56,256]{1,0:T(8,128)S(1)} %get-tuple-element.34.weights, f32[90,56,128]{2,1,0:T(8,128)S(1)} %get-tuple-element.35.dry, ...), custom_call_target="tpu_custom_call" | custom-call | flops 4194304 | bytes 2097152 | tf_op jit(solution)/shard_map/pallas_call | solution.py:313
  27.1 0.0 collective-permute-done.3
  27.1 1.6 %collective-permute-start.4 = (f32[90,128]{1,0:T(8,128)S(1)}, f32[90,128]{1,0:T(8,128)S(1)}, u32[]{:S(2)}, u32[]{:S(2)}) collective-permute-start(f32[90,128]{1,0:T(8,128)S(1)} %add.6), channel_id=1, source_target_pairs={{0,2},{1,3},{2,0},{3,1},{4,6},{5,7},{6,4},{7,5},{8,10},{9,11},{10,... | collective-permute-start | bytes 138248 | tf_op jit(solution)/shard_map/ppermute | solution.py:286
  28.7 2.6 %collective-permute-done.4 = f32[90,128]{1,0:T(8,128)S(1)} collective-permute-done((f32[90,128]{1,0:T(8,128)S(1)}, f32[90,128]{1,0:T(8,128)S(1)}, u32[]{:S(2)}, u32[]{:S(2)}) %collective-permute-start.4) | collective-permute-done | bytes 46112 | tf_op jit(solution)/shard_map/ppermute | solution.py:286
  31.3 0.1 collective-permute-start.5
  31.4 1.2 %collective-permute-done.5.other = f32[90,128]{1,0:T(8,128)S(1)} collective-permute-done((f32[90,128]{1,0:T(8,128)S(1)}, f32[90,128]{1,0:T(8,128)S(1)}, u32[]{:S(2)}, u32[]{:S(2)}) %collective-permute-start.5) | collective-permute-done | bytes 46112 | tf_op jit(solution)/shard_map/ppermute | solution.py:286
  32.6 0.8 %shard_map.136 = (f32[90,1,256]{2,1,0:T(1,128)}, f32[90,1,256]{2,1,0:T(1,128)}) custom-call(f32[90,128]{1,0:T(8,128)S(1)} %add.7.mine, f32[90,128]{1,0:T(8,128)S(1)} %collective-permute-done.5.other, f32[90,1,256]{2,1,0:T(1,128)S(1)} %get-tuple-element.40.temp), custom_call_target="tpu_custom_call" | custom-call | flops 4194304 | bytes 2097152 | tf_op jit(solution)/shard_map/pallas_call | solution.py:324
  (2 shorter events, 0.0 us)
Async XLA Ops:
  2.5 12.7 %collective-permute-start.1 = (f32[184,256]{1,0:T(8,128)S(1)}, f32[184,256]{1,0:T(8,128)S(1)}, u32[]{:S(2)}, u32[]{:S(2)}) collective-permute-start(f32[184,256]{1,0:T(8,128)S(1)} %get-tuple-element.25.fields), channel_id=1, source_target_pairs={{9,1},{11,3},{13,5},{15,7},{0,8},{17,9},{2,10},{19,11},{4,12},{21,... | collective-permute-start | bytes 565256 | tf_op jit(solution)/shard_map/ppermute | solution.py:283
  7.5 7.7 %collective-permute-start = (f32[184,256]{1,0:T(8,128)S(1)}, f32[184,256]{1,0:T(8,128)S(1)}, u32[]{:S(2)}, u32[]{:S(2)}) collective-permute-start(f32[184,256]{1,0:T(8,128)S(1)} %get-tuple-element.25.fields), channel_id=1, source_target_pairs={{5,1},{7,3},{0,4},{9,5},{2,6},{11,7},{4,8},{13,9},{6,10},{15,11},{... | collective-permute-start | bytes 565256 | tf_op jit(solution)/shard_map/ppermute | solution.py:283
  10.9 11.2 %all-to-all-start = ((f32[8,32,128]{2,1,0:T(8,128)}), f32[8,32,128]{2,1,0:T(8,128)S(1)}, u32[]{:S(2)}, u32[]{:S(2)}) async-start(f32[8,32,128]{2,1,0:T(8,128)} %get-tuple-element.30), calls=%async_computation | async-start | bytes 262144 | tf_op jit(solution)/shard_map/all_to_all | solution.py:270
  15.5 7.5 %collective-permute-start.2 = (f32[184,256]{1,0:T(8,128)S(1)}, f32[184,256]{1,0:T(8,128)S(1)}, u32[]{:S(2)}, u32[]{:S(2)}) collective-permute-start(f32[184,256]{1,0:T(8,128)S(1)} %get-tuple-element.29), channel_id=1, source_target_pairs={{0,1},{1,0},{2,3},{3,2},{4,5},{5,4},{6,7},{7,6},{8,9},{9,8},{10,11... | collective-permute-start | bytes 565256 | tf_op jit(solution)/shard_map/ppermute | solution.py:286
  25.1 2.0 %collective-permute-start.3 = (f32[90,128]{1,0:T(8,128)S(1)}, f32[90,128]{1,0:T(8,128)S(1)}, u32[]{:S(2)}, u32[]{:S(2)}) collective-permute-start(f32[90,128]{1,0:T(8,128)S(1)} %get-tuple-element.43), channel_id=1, source_target_pairs={{0,1},{1,0},{2,3},{3,2},{4,5},{5,4},{6,7},{7,6},{8,9},{9,8},{10,11... | collective-permute-start | bytes 138248 | tf_op jit(solution)/shard_map/ppermute | solution.py:286
  27.1 4.2 %collective-permute-start.4 = (f32[90,128]{1,0:T(8,128)S(1)}, f32[90,128]{1,0:T(8,128)S(1)}, u32[]{:S(2)}, u32[]{:S(2)}) collective-permute-start(f32[90,128]{1,0:T(8,128)S(1)} %add.6), channel_id=1, source_target_pairs={{0,2},{1,3},{2,0},{3,1},{4,6},{5,7},{6,4},{7,5},{8,10},{9,11},{10,... | collective-permute-start | bytes 138248 | tf_op jit(solution)/shard_map/ppermute | solution.py:286
  31.3 1.3 %collective-permute-start.5 = (f32[90,128]{1,0:T(8,128)S(1)}, f32[90,128]{1,0:T(8,128)S(1)}, u32[]{:S(2)}, u32[]{:S(2)}) collective-permute-start(f32[90,128]{1,0:T(8,128)S(1)} %add.7.mine), channel_id=1, source_target_pairs={{0,1},{1,0},{2,3},{3,2},{4,5},{5,4},{6,7},{7,6},{8,9},{9,8},{10,11... | collective-permute-start | bytes 138248 | tf_op jit(solution)/shard_map/ppermute | solution.py:286

commit v4 on v3

--- a/solution.py
+++ b/solution.py
@@ -50,13 +50,14 @@
     n_in = kept + 3 + packed
     given, rest = refs[:n_in], refs[n_in:]
     outs, scratch, sems = rest[: 1 + packed + kept], rest[1 + packed + kept : -1], rest[-1]
+    scratch, spare = scratch[: 3 + packed], scratch[3 + packed :]
     targets = tuple(scratch) + tuple(outs[1 + packed :])
     copies = [pltpu.make_async_copy(g, t, sems.at[i]) for i, (g, t) in enumerate(zip(given, targets))]
     for copy in copies:
         copy.start()
     fields = outs[0]
     if packed:
-        factors, blocks = scratch[0], outs[1]
+        factors, blocks = scratch[0], spare[0]
         tiles, rows, _ = blocks.shape
         top = factors.shape[0] - rows
         lane = lax.broadcasted_iota(jnp.int32, (rows, 2 * cap), 1)
@@ -66,6 +67,8 @@
             second = factors[top : top + rows, pair * 2 * cap : (pair + 1) * 2 * cap]
             blocks[2 * pair] = jnp.where(lane < cap, first, pltpu.roll(second, cap, 1))
             blocks[2 * pair + 1] = jnp.where(lane < cap, pltpu.roll(first, cap, 1), second)
+        sending = pltpu.make_async_copy(blocks, outs[1], sems.at[n_in])
+        sending.start()
     kelvin, moisture, spread = scratch[packed:]
     for copy in copies[packed : packed + 3]:
         copy.wait()
@@ -79,10 +82,25 @@
         fields[2 * levels + 1 :, :] = jnp.zeros((left, fields.shape[1]), jnp.float32)
     for copy in copies[packed + 3 :]:
         copy.wait()
-
-
-def prepare_kernel(cap, tiles, levels, owners, fields, choice, base):
+    if packed:
+        sending.wait()
+
+
+def prepare_kernel(cap, tiles, levels, fields, *refs):
+    given, (slot, dry, base), kept, (owners, arid, sems) = refs[:7], refs[7:10], refs[10:15], refs[15:]
+    copies = [
+        pltpu.make_async_copy(g, t, sems.at[i]) for i, (g, t) in enumerate(zip(given, (owners, arid) + kept))
+    ]
+    for copy in copies:
+        copy.start()
+    f = fields[...]
+    spread = fields[2 * levels : 2 * levels + 1, :]
+    f = f + spread * around(f)
+    base[...] = f + spread * around(f)
+    for copy in copies:
+        copy.wait()
     columns = owners.shape[1]
+    gpoints = arid.shape[0]
     owner = owners[...]
     matches = lax.broadcasted_iota(jnp.int32, (tiles, columns), 0) == owner
     member = matches.astype(jnp.float32)
@@ -91,16 +109,12 @@
     earlier = (r < c).astype(jnp.float32).astype(jnp.bfloat16)
     counts = jnp.dot(member.astype(jnp.bfloat16), earlier, preferred_element_type=jnp.float32)
     rank = jnp.sum(jnp.where(matches, counts, 0.0), axis=0, keepdims=True)
-    slot = owner * cap + rank.astype(jnp.int32)
-    chosen = (lax.broadcasted_iota(jnp.int32, (tiles * cap, columns), 0) == slot).astype(jnp.float32)
-    choice[...] = chosen.astype(jnp.bfloat16)
-    f = fields[...]
-    spread = fields[2 * levels : 2 * levels + 1, :]
-    f = f + spread * around(f)
-    base[...] = f + spread * around(f)
-
-
-def select_kernel(cap, tiles, packed, levels, homed, choice, vapour, arid, weights, dry):
+    slot[...] = owner * cap + rank.astype(jnp.int32)
+    for l in range(levels):
+        dry[l] = jnp.broadcast_to(arid[:, l : l + 1] * -LOG2E, (gpoints, dry.shape[2]))
+
+
+def select_kernel(cap, tiles, packed, homed, slot, vapour, weights):
     gpoints = weights.shape[0]
     if packed:
         rows = homed.shape[1]
@@ -115,12 +129,12 @@
         table = jnp.concatenate([lower, upper], axis=0)
     else:
         table = homed[...]
+    chosen = lax.broadcasted_iota(jnp.int32, (tiles * cap, slot.shape[1]), 0) == slot[...]
+    choice = chosen.astype(jnp.float32).astype(jnp.bfloat16)
     picked = 0.0
     for part in split3(table):
-        picked = picked + jnp.dot(part, choice[...], preferred_element_type=jnp.float32)
+        picked = picked + jnp.dot(part, choice, preferred_element_type=jnp.float32)
     weights[...] = picked * (column_of(vapour[...]) * -LOG2E)
-    for l in range(levels):
-        dry[l] = jnp.broadcast_to(arid[:, l : l + 1] * -LOG2E, (gpoints, dry.shape[2]))
 
 
 def side_kernel(levels, fields, near, far, base, share, total):
@@ -141,13 +155,26 @@
         wet[l] = f[levels + l : levels + l + 1]
 
 
+def tree_sum(terms):
+    terms = list(terms)
+    while len(terms) > 1:
+        terms = [sum(terms[i + 1 : i + 2], terms[i]) for i in range(0, len(terms), 2)]
+    return terms[0]
+
+
+def unrolled(levels, most):
+    return max(u for u in range(1, most + 1) if levels % u == 0)
+
+
+UD, UU = 30, 90
+
+
 def radiation_kernel(
-    levels, gpoints, first, temp, wet, weights, dry, angle, lit, black, solar, part, rest, sums
+    levels, gpoints, first, temp, wet, weights, dry, angle, lit, black, solar, part, rest, steps, sums
 ):
     blocks = gpoints // 8
     black_column = jnp.broadcast_to(column_of(black[...]), (gpoints, 128))
     solar_column = jnp.broadcast_to(column_of(solar[...]), (gpoints, 128))
-    unroll = max(u for u in range(1, 11) if levels % u == 0)
     parity = lax.rem(lax.axis_index("grp"), 2)
     half = 1 - parity if first else parity
     at = pl.ds(pl.multiple_of(half * 128, 128), 128)
@@ -157,41 +184,43 @@
     share_of = [black_column[8 * b : 8 * b + 8] for b in range(blocks)]
     weight = [weights[8 * b : 8 * b + 8, at] for b in range(blocks)]
     beams = tuple(solar_column[8 * b : 8 * b + 8] * marker for b in range(blocks))
-    zero = tuple(jnp.zeros((8, 128), jnp.float32) for _ in range(blocks))
+    zero = jnp.zeros((8, 128), jnp.float32)
+
+    def level(l):
+        return pl.ds(pl.multiple_of(l * 8, 8), 8)
 
     def down_level(l, carry):
-        down, beam = carry
+        down, beam, passed = carry
         warm = jnp.broadcast_to(temp[l, :, at], (8, 128))
         moist = jnp.broadcast_to(wet[l, :, at], (8, 128))
-        new_down, new_beam, acc = [], [], None
+        new_down, new_beam = [], []
         for b in range(blocks):
             tau = dry[l, 8 * b : 8 * b + 8, :] + weight[b] * moist
             lost = 1.0 - jnp.exp2(tau)
+            step = lost * (down[b] - warm)
             rest[l, 8 * b : 8 * b + 8, :] = lost
-            step = lost * (down[b] - share_of[b] * warm)
+            steps[l, 8 * b : 8 * b + 8, :] = step
             after = beam[b] * jnp.exp2(tau * inverse)
-            net = step + (beam[b] - after)
-            acc = net if acc is None else acc + net
             new_down.append(down[b] - step)
             new_beam.append(after)
-        sums[pl.ds(pl.multiple_of(l * 8, 8), 8), :] = acc
-        return tuple(new_down), tuple(new_beam)
+        passing = tree_sum(new_beam)
+        sums[level(l), :] = passed - passing
+        return tuple(new_down), tuple(new_beam), passing
 
     def up_level(i, up):
         l = levels - 1 - i
         warm = jnp.broadcast_to(temp[l, :, at], (8, 128))
-        new_up, acc = [], None
+        new_up, terms = [], [sums[level(l), :]]
         for b in range(blocks):
-            step = rest[l, 8 * b : 8 * b + 8, :] * (share_of[b] * warm - up[b])
-            acc = step if acc is None else acc + step
-            new_up.append(up[b] + step)
-        where = pl.ds(pl.multiple_of(l * 8, 8), 8)
-        sums[where, :] = sums[where, :] - acc
+            step = rest[l, 8 * b : 8 * b + 8, :] * (up[b] - warm)
+            terms.append(share_of[b] * (step + steps[l, 8 * b : 8 * b + 8, :]))
+            new_up.append(up[b] - step)
+        sums[level(l), :] = tree_sum(terms)
         return tuple(new_up)
 
-    lax.fori_loop(0, levels, down_level, (zero, beams), unroll=unroll)
+    lax.fori_loop(0, levels, down_level, ((zero,) * blocks, beams, tree_sum(beams)), unroll=unrolled(levels, UD))
     floor = jnp.broadcast_to(temp[levels - 1, :, at], (8, 128))
-    lax.fori_loop(0, levels, up_level, tuple(s * floor for s in share_of), unroll=unroll)
+    lax.fori_loop(0, levels, up_level, (floor,) * blocks, unroll=unrolled(levels, UU))
     total = sums[pl.ds(0, levels, stride=8), :]
     for s in range(1, 8):
         total = total + sums[pl.ds(s, levels, stride=8), :]
@@ -206,12 +235,12 @@
 
 
 def second_half_kernel(
-    levels, gpoints, temp, wet, weights, dry, angle, lit, black, solar, part, vapour, rest, sums, sem
+    levels, gpoints, temp, wet, weights, dry, angle, lit, black, solar, part, vapour, rest, steps, sums, sem
 ):
     copy = pltpu.make_async_copy(wet, vapour, sem)
     copy.start()
     radiation_kernel(
-        levels, gpoints, False, temp, wet, weights, dry, angle, lit, black, solar, part, rest, sums
+        levels, gpoints, False, temp, wet, weights, dry, angle, lit, black, solar, part, rest, steps, sums
     )
     copy.wait()
 
@@ -253,19 +282,20 @@
     half = (gpoints + 8) // 2
     inputs = [factors] * packed + [kelvin, moisture, spreading_number]
     row = (1, gpoints)
-    small = [owners.reshape(1, width), vapour_absorption.reshape(row), arid]
+    small = [owners.reshape(1, width), arid, vapour_absorption.reshape(row)]
     small += [angle, lit, black.reshape(row), solar.reshape(row)]
     outs = [jax.ShapeDtypeStruct((stacked, width), jnp.float32)]
     outs += [jax.ShapeDtypeStruct((n_tile, half, 128), jnp.float32)] * packed
     results = kernel_call(
-        functools.partial(pack_kernel, cap, packed, len(small)),
-        outs + [jax.ShapeDtypeStruct(v.shape, v.dtype) for v in small],
+        functools.partial(pack_kernel, cap, packed, 0),
+        outs,
         scratch=[pltpu.VMEM(v.shape, v.dtype) for v in inputs]
-        + [pltpu.SemaphoreType.DMA((len(inputs) + len(small),))],
-        in_specs=[FAR] * (len(inputs) + len(small)),
-    )(*(pltpu.with_memory_space_constraint(v, pltpu.HBM) for v in inputs + small))
+        + [pltpu.VMEM((n_tile, half, 128), jnp.float32)] * packed
+        + [pltpu.SemaphoreType.DMA((len(inputs) + packed,))],
+        in_specs=[FAR] * len(inputs),
+        out_specs=[VM] + [FAR] * packed,
+    )(*(pltpu.with_memory_space_constraint(v, pltpu.HBM) for v in inputs))
     fields = results[0]
-    owners, vapour_absorption, arid, angle, lit, black, solar = results[1 + packed :]
     if packed:
         homed = lax.all_to_all(results[1], "tile", split_axis=0, concat_axis=0, tiled=True)
     else:
@@ -287,20 +317,22 @@
 
     near = from_side(1)
     far = from_side(2)
-    choice, base = kernel_call(
+    slot, dry, base, vapour_absorption, angle, lit, black, solar = kernel_call(
         functools.partial(prepare_kernel, cap, n_tile, levels),
-        [jax.ShapeDtypeStruct((slots, width), jnp.bfloat16), (stacked, width)],
-    )(owners, fields)
-    weights, dry = kernel_call(
-        functools.partial(select_kernel, cap, n_tile, packed, levels),
-        [(gpoints, width), (levels, gpoints, 128)],
-    )(homed, choice, vapour_absorption, arid)
-    share, mine = kernel_call(
-        functools.partial(side_kernel, levels), [(stacked, width)] * 2
-    )(fields, near, far, base)
+        [jax.ShapeDtypeStruct((1, width), jnp.int32), (levels, gpoints, 128), (stacked, width)]
+        + [jax.ShapeDtypeStruct(v.shape, v.dtype) for v in small[2:]],
+        scratch=[pltpu.VMEM(v.shape, v.dtype) for v in small[:2]]
+        + [pltpu.SemaphoreType.DMA((len(small),))],
+        in_specs=[VM] + [FAR] * len(small),
+    )(fields, *(pltpu.with_memory_space_constraint(v, pltpu.HBM) for v in small))
+    (weights,) = kernel_call(
+        functools.partial(select_kernel, cap, n_tile, packed), [(gpoints, width)]
+    )(homed, slot, vapour_absorption)
+    share, mine = kernel_call(functools.partial(side_kernel, levels), [(stacked, width)] * 2)(fields, near, far, base)
     other = swapped(share, 1)
     tables = (weights, dry, angle, lit, black, solar)
     work = [
+        pltpu.VMEM((levels, gpoints, 128), jnp.float32),
         pltpu.VMEM((levels, gpoints, 128), jnp.float32),
         pltpu.VMEM((levels * 8, 128), jnp.float32),
     ]

time: 33.7 us -> 32.2 us (0.955)
  waiting for transfers between devices: 10.4 us -> 8.31 us
  Pallas kernels: 8.2 us -> 8.87 us
    all_to_all x1, waiting for transfers between devices: 6.51 us -> 4.43 us  [on_device(): lax.all_to_all(results[1], 'tile', split_axis=0, concat_axis=0, tiled=True)]
    pallas_call x1, Pallas kernels: 0.4 us -> 1.9 us  [on_device(): kernel_call(functools.partial(prepare_kernel, cap, n_tile, levels), [jax....]
    pallas_call x2, Pallas kernels: 2.8 us -> 1.96 us  [the longest x1 1.68 us: on_device(): kernel_call(functools.partial(pack_kernel, cap, packed, 0), outs, scratch...]
    pallas_call x1, Pallas kernels: 0.31 us -> 0.98 us  [on_device(): kernel_call(functools.partial(side_kernel, levels), [(stacked, width)] * 2)]
  transfers between devices with their start and end apart: 7 -> 7, of which waited for: 3 -> 3; matrix products, arithmetic and copies ran while one was open for 0% -> 0% of each run, Pallas kernels for 11% -> 15%
where the time goes in v4:
time: 32.2 us; the launch traced here: 31.9 us
  starting transfers between devices  14 us (43%)
  Pallas kernels  8.87 us (28%)
  waiting for transfers between devices  8.31 us (26%)
  between operations  0.74 us (2%)
    ppermute x2, starting transfers between devices, from_side(): return lax.ppermute(fields, ('tile', 'grp'), pairs)  8.4 us
    all_to_all x1, waiting for transfers between devices, on_device(): lax.all_to_all(results[1], 'tile', split_axis=0, concat_axis=0, tiled=True)  4.43 us
    ppermute x4, waiting for transfers between devices, swapped(): return lax.ppermute(x, 'grp', [(i, i ^ bit) for i in range(n_grp)])  3.87 us
    all_to_all x1, starting transfers between devices, on_device(): lax.all_to_all(results[1], 'tile', split_axis=0, concat_axis=0, tiled=True)  3.86 us
    pallas_call x1, Pallas kernels, on_device(): kernel_call(functools.partial(prepare_kernel, cap, n_tile, levels), [jax....  1.9 us
    ppermute x4, starting transfers between devices, swapped(): return lax.ppermute(x, 'grp', [(i, i ^ bit) for i in range(n_grp)])  1.7 us
    pallas_call x1, Pallas kernels, on_device(): kernel_call(functools.partial(pack_kernel, cap, packed, 0), outs, scratch...  1.68 us
    pallas_call x1, Pallas kernels, on_device(): kernel_call(functools.partial(first_half_kernel, levels, gpoints), [(leve...  1.65 us
  transfers between devices with their start and end apart: 7, of which 3 were waited for; matrix products, arithmetic and copies ran while one was open for 0% of the time, Pallas kernels for 15%

profile of v4, /device:TPU:0, one launch (start us, length us, event | category | flops | bytes accessed | tf_op | source)
XLA Modules:
  0.0 31.9 jit_solution(9171588541281971316)
XLA Ops:
  0.6 1.7 %shard_map.130 = (f32[184,256]{1,0:T(8,128)S(1)}, f32[8,32,128]{2,1,0:T(8,128)}) custom-call(f32[56,512]{1,0:T(8,128)} %refs_0_.1, f32[90,1,256]{2,1,0:T(1,128)} %refs_1_.2, f32[90,1,256]{2,1,0:T(1,128)} %refs_2_.1, f32[1,256]{1,0:T(1,128)} %refs_3_.2), custom_call_target="tpu_custom_call" | custom-call | flops 4194304 | bytes 2097152 | tf_op jit(solution)/shard_map/pallas_call | solution.py:289
  2.3 5.0 %collective-permute-start.1 = (f32[184,256]{1,0:T(8,128)S(1)}, f32[184,256]{1,0:T(8,128)S(1)}, u32[]{:S(2)}, u32[]{:S(2)}) collective-permute-start(f32[184,256]{1,0:T(8,128)S(1)} %get-tuple-element.22.fields), channel_id=1, source_target_pairs={{9,1},{11,3},{13,5},{15,7},{0,8},{17,9},{2,10},{19,11},{4,12},{21,... | collective-permute-start | bytes 565256 | tf_op jit(solution)/shard_map/ppermute | solution.py:313
  7.3 3.4 %collective-permute-start = (f32[184,256]{1,0:T(8,128)S(1)}, f32[184,256]{1,0:T(8,128)S(1)}, u32[]{:S(2)}, u32[]{:S(2)}) collective-permute-start(f32[184,256]{1,0:T(8,128)S(1)} %get-tuple-element.22.fields), channel_id=1, source_target_pairs={{5,1},{7,3},{0,4},{9,5},{2,6},{11,7},{4,8},{13,9},{6,10},{15,11},{... | collective-permute-start | bytes 565256 | tf_op jit(solution)/shard_map/ppermute | solution.py:313
  10.7 3.9 %all-to-all-start = ((f32[8,32,128]{2,1,0:T(8,128)}), f32[8,32,128]{2,1,0:T(8,128)S(1)}, u32[]{:S(2)}, u32[]{:S(2)}) async-start(f32[8,32,128]{2,1,0:T(8,128)} %get-tuple-element.26), calls=%async_computation | async-start | bytes 262144 | tf_op jit(solution)/shard_map/all_to_all | solution.py:300
  14.6 1.9 %shard_map.131 = (s32[1,256]{1,0:T(1,128)S(1)}, f32[90,56,128]{2,1,0:T(8,128)S(1)}, f32[184,256]{1,0:T(8,128)S(1)}, f32[1,56]{1,0:T(1,128)S(1)}, f32[1,256]{1,0:...) custom-call(f32[184,256]{1,0:T(8,128)S(1)} %get-tuple-element.22.fields, ...), custom_call_target="tpu_custom_call" | custom-call | flops 4194304 | bytes 2097152 | tf_op jit(solution)/shard_map/pallas_call | solution.py:320
  16.5 0.0 collective-permute-done.1.far
  16.5 0.0 collective-permute-done.near
  16.5 1.0 %shard_map.132 = (f32[184,256]{1,0:T(8,128)}, f32[184,256]{1,0:T(8,128)S(1)}) custom-call(f32[184,256]{1,0:T(8,128)S(1)} %get-tuple-element.22.fields, f32[184,256]{1,0:T(8,128)S(1)} %collective-permute-done.near, f32[184,256]{1,0:T(8,128)S(1)} %collective-permute-done.1.far, f32[184,256]{1,0:T(8,128)S(1)} %get-tuple-element.23.base), custom_call_target="tpu_custom_call" | custom-call | flops 4194304 | bytes 2097152 | tf_op jit(solution)/shard_map/pallas_call | solution.py:331
  17.5 0.0 collective-permute-start.2
  17.5 4.4 %all-to-all-done.homed = f32[8,32,128]{2,1,0:T(8,128)S(1)} async-done(((f32[8,32,128]{2,1,0:T(8,128)}), f32[8,32,128]{2,1,0:T(8,128)S(1)}, u32[]{:S(2)}, u32[]{:S(2)}) %all-to-all-start) | async-done | bytes 131104 | tf_op jit(solution)/shard_map/all_to_all | solution.py:300
  21.9 0.3 shard_map.133.weights
  22.2 0.0 collective-permute-done.2.share
  22.2 1.7 %shard_map.134 = (f32[90,128]{1,0:T(8,128)S(1)}, f32[90,1,256]{2,1,0:T(1,128)S(1)}, f32[90,1,256]{2,1,0:T(1,128)S(1)}) custom-call(f32[184,256]{1,0:T(8,128)S(1)} %get-tuple-element.24.base, f32[184,256]{1,0:T(8,128)S(1)} %collective-permute-done.2.share, f32[56,256]{1,0:T(8,128)S(1)} %shard_map.133.weights, f32[90,56,128]{2,1,0:T(8,128)S(1)} %get-tuple-element.29.dry, ...), custom_call_target="tpu_custom_call" | custom-call | flops 4194304 | bytes 2097152 | tf_op jit(solution)/shard_map/pallas_call | solution.py:339
  23.9 0.1 collective-permute-start.3
  24.0 1.6 %shard_map.135 = (f32[90,128]{1,0:T(8,128)S(1)}, f32[90,1,256]{2,1,0:T(1,128)}) custom-call(f32[90,1,256]{2,1,0:T(1,128)S(1)} %get-tuple-element.34.temp, f32[90,1,256]{2,1,0:T(1,128)S(1)} %get-tuple-element.35.wet, f32[56,256]{1,0:T(8,128)S(1)} %shard_map.133.weights, f32[90,56,128]{2,1,0:T(8,128)S(1)} %get-tuple-element.29.dry, ...), custom_call_target="tpu_custom_call" | custom-call | flops 4194304 | bytes 2097152 | tf_op jit(solution)/shard_map/pallas_call | solution.py:345
  25.6 0.0 collective-permute-done.3
  25.6 1.6 %collective-permute-start.4 = (f32[90,128]{1,0:T(8,128)S(1)}, f32[90,128]{1,0:T(8,128)S(1)}, u32[]{:S(2)}, u32[]{:S(2)}) collective-permute-start(f32[90,128]{1,0:T(8,128)S(1)} %add.6), channel_id=1, source_target_pairs={{0,2},{1,3},{2,0},{3,1},{4,6},{5,7},{6,4},{7,5},{8,10},{9,11},{10,... | collective-permute-start | bytes 138248 | tf_op jit(solution)/shard_map/ppermute | solution.py:316
  27.2 2.6 %collective-permute-done.4 = f32[90,128]{1,0:T(8,128)S(1)} collective-permute-done((f32[90,128]{1,0:T(8,128)S(1)}, f32[90,128]{1,0:T(8,128)S(1)}, u32[]{:S(2)}, u32[]{:S(2)}) %collective-permute-start.4) | collective-permute-done | bytes 46112 | tf_op jit(solution)/shard_map/ppermute | solution.py:316
  29.8 0.1 collective-permute-start.5
  29.9 1.2 %collective-permute-done.5.other = f32[90,128]{1,0:T(8,128)S(1)} collective-permute-done((f32[90,128]{1,0:T(8,128)S(1)}, f32[90,128]{1,0:T(8,128)S(1)}, u32[]{:S(2)}, u32[]{:S(2)}) %collective-permute-start.5) | collective-permute-done | bytes 46112 | tf_op jit(solution)/shard_map/ppermute | solution.py:316
  31.1 0.8 %shard_map.136 = (f32[90,1,256]{2,1,0:T(1,128)}, f32[90,1,256]{2,1,0:T(1,128)}) custom-call(f32[90,128]{1,0:T(8,128)S(1)} %add.7.mine, f32[90,128]{1,0:T(8,128)S(1)} %collective-permute-done.5.other, f32[90,1,256]{2,1,0:T(1,128)S(1)} %get-tuple-element.34.temp), custom_call_target="tpu_custom_call" | custom-call | flops 4194304 | bytes 2097152 | tf_op jit(solution)/shard_map/pallas_call | solution.py:356
  (2 shorter events, 0.0 us)
Async XLA Ops:
  2.3 14.2 %collective-permute-start.1 = (f32[184,256]{1,0:T(8,128)S(1)}, f32[184,256]{1,0:T(8,128)S(1)}, u32[]{:S(2)}, u32[]{:S(2)}) collective-permute-start(f32[184,256]{1,0:T(8,128)S(1)} %get-tuple-element.22.fields), channel_id=1, source_target_pairs={{9,1},{11,3},{13,5},{15,7},{0,8},{17,9},{2,10},{19,11},{4,12},{21,... | collective-permute-start | bytes 565256 | tf_op jit(solution)/shard_map/ppermute | solution.py:313
  7.3 9.2 %collective-permute-start = (f32[184,256]{1,0:T(8,128)S(1)}, f32[184,256]{1,0:T(8,128)S(1)}, u32[]{:S(2)}, u32[]{:S(2)}) collective-permute-start(f32[184,256]{1,0:T(8,128)S(1)} %get-tuple-element.22.fields), channel_id=1, source_target_pairs={{5,1},{7,3},{0,4},{9,5},{2,6},{11,7},{4,8},{13,9},{6,10},{15,11},{... | collective-permute-start | bytes 565256 | tf_op jit(solution)/shard_map/ppermute | solution.py:313
  10.7 11.2 %all-to-all-start = ((f32[8,32,128]{2,1,0:T(8,128)}), f32[8,32,128]{2,1,0:T(8,128)S(1)}, u32[]{:S(2)}, u32[]{:S(2)}) async-start(f32[8,32,128]{2,1,0:T(8,128)} %get-tuple-element.26), calls=%async_computation | async-start | bytes 262144 | tf_op jit(solution)/shard_map/all_to_all | solution.py:300
  17.5 4.7 %collective-permute-start.2 = (f32[184,256]{1,0:T(8,128)}, f32[184,256]{1,0:T(8,128)S(1)}, u32[]{:S(2)}, u32[]{:S(2)}) collective-permute-start(f32[184,256]{1,0:T(8,128)} %get-tuple-element.25), channel_id=1, source_target_pairs={{0,1},{1,0},{2,3},{3,2},{4,5},{5,4},{6,7},{7,6},{8,9},{9,8},{10,11... | collective-permute-start | bytes 565256 | tf_op jit(solution)/shard_map/ppermute | solution.py:316
  23.9 1.7 %collective-permute-start.3 = (f32[90,128]{1,0:T(8,128)S(1)}, f32[90,128]{1,0:T(8,128)S(1)}, u32[]{:S(2)}, u32[]{:S(2)}) collective-permute-start(f32[90,128]{1,0:T(8,128)S(1)} %get-tuple-element.37), channel_id=1, source_target_pairs={{0,1},{1,0},{2,3},{3,2},{4,5},{5,4},{6,7},{7,6},{8,9},{9,8},{10,11... | collective-permute-start | bytes 138248 | tf_op jit(solution)/shard_map/ppermute | solution.py:316
  25.6 4.2 %collective-permute-start.4 = (f32[90,128]{1,0:T(8,128)S(1)}, f32[90,128]{1,0:T(8,128)S(1)}, u32[]{:S(2)}, u32[]{:S(2)}) collective-permute-start(f32[90,128]{1,0:T(8,128)S(1)} %add.6), channel_id=1, source_target_pairs={{0,2},{1,3},{2,0},{3,1},{4,6},{5,7},{6,4},{7,5},{8,10},{9,11},{10,... | collective-permute-start | bytes 138248 | tf_op jit(solution)/shard_map/ppermute | solution.py:316
  29.8 1.3 %collective-permute-start.5 = (f32[90,128]{1,0:T(8,128)S(1)}, f32[90,128]{1,0:T(8,128)S(1)}, u32[]{:S(2)}, u32[]{:S(2)}) collective-permute-start(f32[90,128]{1,0:T(8,128)S(1)} %add.7.mine), channel_id=1, source_target_pairs={{0,1},{1,0},{2,3},{3,2},{4,5},{5,4},{6,7},{7,6},{8,9},{9,8},{10,11... | collective-permute-start | bytes 138248 | tf_op jit(solution)/shard_map/ppermute | solution.py:316

commit v5 on v4

--- a/solution.py
+++ b/solution.py
@@ -86,8 +86,8 @@
         sending.wait()
 
 
-def prepare_kernel(cap, tiles, levels, fields, *refs):
-    given, (slot, dry, base), kept, (owners, arid, sems) = refs[:7], refs[7:10], refs[10:15], refs[15:]
+def prepare_kernel(cap, tiles, levels, fields, near, *refs):
+    given, (slot, dry, base, part), kept, (owners, arid, sems) = refs[:7], refs[7:11], refs[11:16], refs[16:]
     copies = [
         pltpu.make_async_copy(g, t, sems.at[i]) for i, (g, t) in enumerate(zip(given, (owners, arid) + kept))
     ]
@@ -95,8 +95,12 @@
         copy.start()
     f = fields[...]
     spread = fields[2 * levels : 2 * levels + 1, :]
-    f = f + spread * around(f)
-    base[...] = f + spread * around(f)
+    first = f + spread * around(f)
+    n = near[...]
+    v = spread * n
+    side = v + spread * (around(v) + n + near[2 * levels : 2 * levels + 1, :] * (f + around(n)))
+    part[...] = side
+    base[...] = first + spread * around(first) + side
     for copy in copies:
         copy.wait()
     columns = owners.shape[1]
@@ -137,15 +141,11 @@
     weights[...] = picked * (column_of(vapour[...]) * -LOG2E)
 
 
-def side_kernel(levels, fields, near, far, base, share, total):
-    spread = fields[2 * levels : 2 * levels + 1, :]
-    near_spread = near[2 * levels : 2 * levels + 1, :]
-    f = near[...]
-    near_next = f + near_spread * (far[...] + fields[...] + around(f))
-    v = spread * f
-    part = v + spread * (around(v) + near_next)
-    share[...] = part
-    total[...] = base[...] + part
+def side_kernel(levels, fields, near, far, base, part, share, total):
+    row = slice(2 * levels, 2 * levels + 1)
+    add = (fields[row, :] * near[row, :]) * far[...]
+    share[...] = part[...] + add
+    total[...] = base[...] + add
 
 
 def spread_rows(levels, base, share, temp, wet):
@@ -190,37 +190,39 @@
         return pl.ds(pl.multiple_of(l * 8, 8), 8)
 
     def down_level(l, carry):
-        down, beam, passed = carry
+        down, beam = carry
         warm = jnp.broadcast_to(temp[l, :, at], (8, 128))
         moist = jnp.broadcast_to(wet[l, :, at], (8, 128))
+        sums[level(l), :] = tree_sum(beam)
         new_down, new_beam = [], []
         for b in range(blocks):
             tau = dry[l, 8 * b : 8 * b + 8, :] + weight[b] * moist
-            lost = 1.0 - jnp.exp2(tau)
-            step = lost * (down[b] - warm)
-            rest[l, 8 * b : 8 * b + 8, :] = lost
-            steps[l, 8 * b : 8 * b + 8, :] = step
-            after = beam[b] * jnp.exp2(tau * inverse)
-            new_down.append(down[b] - step)
-            new_beam.append(after)
-        passing = tree_sum(new_beam)
-        sums[level(l), :] = passed - passing
-        return tuple(new_down), tuple(new_beam), passing
-
-    def up_level(i, up):
+            kept = jnp.exp2(tau)
+            rest[l, 8 * b : 8 * b + 8, :] = kept
+            steps[l, 8 * b : 8 * b + 8, :] = down[b]
+            new_beam.append(beam[b] * jnp.exp2(tau * inverse))
+            new_down.append(warm + kept * (down[b] - warm))
+        return tuple(new_down), tuple(new_beam)
+
+    def up_level(i, carry):
+        up, below = carry
         l = levels - 1 - i
         warm = jnp.broadcast_to(temp[l, :, at], (8, 128))
         new_up, terms = [], [sums[level(l), :]]
         for b in range(blocks):
-            step = rest[l, 8 * b : 8 * b + 8, :] * (up[b] - warm)
-            terms.append(share_of[b] * (step + steps[l, 8 * b : 8 * b + 8, :]))
-            new_up.append(up[b] - step)
-        sums[level(l), :] = tree_sum(terms)
-        return tuple(new_up)
-
-    lax.fori_loop(0, levels, down_level, ((zero,) * blocks, beams, tree_sum(beams)), unroll=unrolled(levels, UD))
+            u = warm + rest[l, 8 * b : 8 * b + 8, :] * (up[b] - warm)
+            terms.append(share_of[b] * (steps[l, 8 * b : 8 * b + 8, :] - u))
+            new_up.append(u)
+        flux = tree_sum(terms)
+        sums[level(l), :] = flux - below
+        return tuple(new_up), flux
+
+    down, beam = lax.fori_loop(
+        0, levels, down_level, ((zero,) * blocks, beams), unroll=unrolled(levels, UD)
+    )
     floor = jnp.broadcast_to(temp[levels - 1, :, at], (8, 128))
-    lax.fori_loop(0, levels, up_level, (floor,) * blocks, unroll=unrolled(levels, UU))
+    ground = tree_sum([s * (d - floor) for s, d in zip(share_of, down)] + list(beam))
+    lax.fori_loop(0, levels, up_level, ((floor,) * blocks, ground), unroll=unrolled(levels, UU))
     total = sums[pl.ds(0, levels, stride=8), :]
     for s in range(1, 8):
         total = total + sums[pl.ds(s, levels, stride=8), :]
@@ -317,18 +319,21 @@
 
     near = from_side(1)
     far = from_side(2)
-    slot, dry, base, vapour_absorption, angle, lit, black, solar = kernel_call(
+    slot, dry, base, side, vapour_absorption, angle, lit, black, solar = kernel_call(
         functools.partial(prepare_kernel, cap, n_tile, levels),
-        [jax.ShapeDtypeStruct((1, width), jnp.int32), (levels, gpoints, 128), (stacked, width)]
+        [jax.ShapeDtypeStruct((1, width), jnp.int32), (levels, gpoints, 128)]
+        + [(stacked, width)] * 2
         + [jax.ShapeDtypeStruct(v.shape, v.dtype) for v in small[2:]],
         scratch=[pltpu.VMEM(v.shape, v.dtype) for v in small[:2]]
         + [pltpu.SemaphoreType.DMA((len(small),))],
-        in_specs=[VM] + [FAR] * len(small),
-    )(fields, *(pltpu.with_memory_space_constraint(v, pltpu.HBM) for v in small))
+        in_specs=[VM] * 2 + [FAR] * len(small),
+    )(fields, near, *(pltpu.with_memory_space_constraint(v, pltpu.HBM) for v in small))
     (weights,) = kernel_call(
         functools.partial(select_kernel, cap, n_tile, packed), [(gpoints, width)]
     )(homed, slot, vapour_absorption)
-    share, mine = kernel_call(functools.partial(side_kernel, levels), [(stacked, width)] * 2)(fields, near, far, base)
+    share, mine = kernel_call(
+        functools.partial(side_kernel, levels), [(stacked, width)] * 2
+    )(fields, near, far, base, side)
     other = swapped(share, 1)
     tables = (weights, dry, angle, lit, black, solar)
     work = [

time: 32.2 us -> 32.1 us (level)
  no operation moved by 1% of the time
where the time goes in v5:
time: 32.1 us; the launch traced here: 31.7 us
  starting transfers between devices  14 us (44%)
  Pallas kernels  8.71 us (27%)
  waiting for transfers between devices  8.3 us (26%)
  between operations  0.74 us (2%)
    ppermute x2, starting transfers between devices, from_side(): return lax.ppermute(fields, ('tile', 'grp'), pairs)  8.4 us
    all_to_all x1, waiting for transfers between devices, on_device(): lax.all_to_all(results[1], 'tile', split_axis=0, concat_axis=0, tiled=True)  4.43 us
    ppermute x4, waiting for transfers between devices, swapped(): return lax.ppermute(x, 'grp', [(i, i ^ bit) for i in range(n_grp)])  3.87 us
    all_to_all x1, starting transfers between devices, on_device(): lax.all_to_all(results[1], 'tile', split_axis=0, concat_axis=0, tiled=True)  3.87 us
    pallas_call x1, Pallas kernels, on_device(): kernel_call(functools.partial(prepare_kernel, cap, n_tile, levels), [jax....  2.19 us
    ppermute x4, starting transfers between devices, swapped(): return lax.ppermute(x, 'grp', [(i, i ^ bit) for i in range(n_grp)])  1.7 us
    pallas_call x1, Pallas kernels, on_device(): kernel_call(functools.partial(pack_kernel, cap, packed, 0), outs, scratch...  1.68 us
    pallas_call x1, Pallas kernels, on_device(): kernel_call(functools.partial(first_half_kernel, levels, gpoints), [(leve...  1.57 us
  transfers between devices with their start and end apart: 7, of which 3 were waited for; matrix products, arithmetic and copies ran while one was open for 0% of the time, Pallas kernels for 15%

profile of v5, /device:TPU:0, one launch (start us, length us, event | category | flops | bytes accessed | tf_op | source)
XLA Modules:
  0.0 31.7 jit_solution(11302305244138373201)
XLA Ops:
  0.6 1.7 %shard_map.130 = (f32[184,256]{1,0:T(8,128)S(1)}, f32[8,32,128]{2,1,0:T(8,128)}) custom-call(f32[56,512]{1,0:T(8,128)} %refs_0_.1, f32[90,1,256]{2,1,0:T(1,128)} %refs_1_.2, f32[90,1,256]{2,1,0:T(1,128)} %refs_2_.1, f32[1,256]{1,0:T(1,128)} %refs_3_.2), custom_call_target="tpu_custom_call" | custom-call | flops 4194304 | bytes 2097152 | tf_op jit(solution)/shard_map/pallas_call | solution.py:291
  2.3 4.9 %collective-permute-start = (f32[184,256]{1,0:T(8,128)S(1)}, f32[184,256]{1,0:T(8,128)S(1)}, u32[]{:S(2)}, u32[]{:S(2)}) collective-permute-start(f32[184,256]{1,0:T(8,128)S(1)} %get-tuple-element.23.fields), channel_id=1, source_target_pairs={{5,1},{7,3},{0,4},{9,5},{2,6},{11,7},{4,8},{13,9},{6,10},{15,11},{... | collective-permute-start | bytes 565256 | tf_op jit(solution)/shard_map/ppermute | solution.py:315
  7.2 3.5 %collective-permute-start.1 = (f32[184,256]{1,0:T(8,128)S(1)}, f32[184,256]{1,0:T(8,128)S(1)}, u32[]{:S(2)}, u32[]{:S(2)}) collective-permute-start(f32[184,256]{1,0:T(8,128)S(1)} %get-tuple-element.23.fields), channel_id=1, source_target_pairs={{9,1},{11,3},{13,5},{15,7},{0,8},{17,9},{2,10},{19,11},{4,12},{21,... | collective-permute-start | bytes 565256 | tf_op jit(solution)/shard_map/ppermute | solution.py:315
  10.7 3.9 %all-to-all-start = ((f32[8,32,128]{2,1,0:T(8,128)}), f32[8,32,128]{2,1,0:T(8,128)S(1)}, u32[]{:S(2)}, u32[]{:S(2)}) async-start(f32[8,32,128]{2,1,0:T(8,128)} %get-tuple-element.28), calls=%async_computation | async-start | bytes 262144 | tf_op jit(solution)/shard_map/all_to_all | solution.py:302
  14.6 0.0 collective-permute-done.near
  14.6 2.2 %shard_map.131 = (s32[1,256]{1,0:T(1,128)S(1)}, f32[90,56,128]{2,1,0:T(8,128)S(1)}, f32[184,256]{1,0:T(8,128)S(1)}, f32[184,256]{1,0:T(8,128)S(1)}, f32[1,56]{1,...) custom-call(f32[184,256]{1,0:T(8,128)S(1)} %get-tuple-element.23.fields, ...), custom_call_target="tpu_custom_call" | custom-call | flops 4194304 | bytes 2097152 | tf_op jit(solution)/shard_map/pallas_call | solution.py:322
  16.8 0.0 collective-permute-done.1.far
  16.8 0.7 %shard_map.132 = (f32[184,256]{1,0:T(8,128)}, f32[184,256]{1,0:T(8,128)S(1)}) custom-call(f32[184,256]{1,0:T(8,128)S(1)} %get-tuple-element.23.fields, f32[184,256]{1,0:T(8,128)S(1)} %collective-permute-done.near, f32[184,256]{1,0:T(8,128)S(1)} %collective-permute-done.1.far, f32[184,256]{1,0:T(8,128)S(1)} %get-tuple-element.24.base, ...), custom_call_target="tpu_custom_call" | custom-call | flops 4194304 | bytes 2097152 | tf_op jit(solution)/shard_map/pallas_call | solution.py:334
  17.5 0.0 collective-permute-start.2
  17.5 4.4 %all-to-all-done.homed = f32[8,32,128]{2,1,0:T(8,128)S(1)} async-done(((f32[8,32,128]{2,1,0:T(8,128)}), f32[8,32,128]{2,1,0:T(8,128)S(1)}, u32[]{:S(2)}, u32[]{:S(2)}) %all-to-all-start) | async-done | bytes 131104 | tf_op jit(solution)/shard_map/all_to_all | solution.py:302
  21.9 0.3 shard_map.133.weights
  22.2 0.0 collective-permute-done.2.share
  22.2 1.6 %shard_map.134 = (f32[90,128]{1,0:T(8,128)S(1)}, f32[90,1,256]{2,1,0:T(1,128)S(1)}, f32[90,1,256]{2,1,0:T(1,128)S(1)}) custom-call(f32[184,256]{1,0:T(8,128)S(1)} %get-tuple-element.26.base, f32[184,256]{1,0:T(8,128)S(1)} %collective-permute-done.2.share, f32[56,256]{1,0:T(8,128)S(1)} %shard_map.133.weights, f32[90,56,128]{2,1,0:T(8,128)S(1)} %get-tuple-element.31.dry, ...), custom_call_target="tpu_custom_call" | custom-call | flops 4194304 | bytes 2097152 | tf_op jit(solution)/shard_map/pallas_call | solution.py:344
  23.8 0.1 collective-permute-start.3
  23.9 1.5 %shard_map.135 = (f32[90,128]{1,0:T(8,128)S(1)}, f32[90,1,256]{2,1,0:T(1,128)}) custom-call(f32[90,1,256]{2,1,0:T(1,128)S(1)} %get-tuple-element.36.temp, f32[90,1,256]{2,1,0:T(1,128)S(1)} %get-tuple-element.37.wet, f32[56,256]{1,0:T(8,128)S(1)} %shard_map.133.weights, f32[90,56,128]{2,1,0:T(8,128)S(1)} %get-tuple-element.31.dry, ...), custom_call_target="tpu_custom_call" | custom-call | flops 4194304 | bytes 2097152 | tf_op jit(solution)/shard_map/pallas_call | solution.py:350
  25.4 0.0 collective-permute-done.3
  25.4 1.6 %collective-permute-start.4 = (f32[90,128]{1,0:T(8,128)S(1)}, f32[90,128]{1,0:T(8,128)S(1)}, u32[]{:S(2)}, u32[]{:S(2)}) collective-permute-start(f32[90,128]{1,0:T(8,128)S(1)} %add.6), channel_id=1, source_target_pairs={{0,2},{1,3},{2,0},{3,1},{4,6},{5,7},{6,4},{7,5},{8,10},{9,11},{10,... | collective-permute-start | bytes 138248 | tf_op jit(solution)/shard_map/ppermute | solution.py:318
  27.0 2.6 %collective-permute-done.4 = f32[90,128]{1,0:T(8,128)S(1)} collective-permute-done((f32[90,128]{1,0:T(8,128)S(1)}, f32[90,128]{1,0:T(8,128)S(1)}, u32[]{:S(2)}, u32[]{:S(2)}) %collective-permute-start.4) | collective-permute-done | bytes 46112 | tf_op jit(solution)/shard_map/ppermute | solution.py:318
  29.7 0.1 collective-permute-start.5
  29.7 1.2 %collective-permute-done.5.other = f32[90,128]{1,0:T(8,128)S(1)} collective-permute-done((f32[90,128]{1,0:T(8,128)S(1)}, f32[90,128]{1,0:T(8,128)S(1)}, u32[]{:S(2)}, u32[]{:S(2)}) %collective-permute-start.5) | collective-permute-done | bytes 46112 | tf_op jit(solution)/shard_map/ppermute | solution.py:318
  31.0 0.8 %shard_map.136 = (f32[90,1,256]{2,1,0:T(1,128)}, f32[90,1,256]{2,1,0:T(1,128)}) custom-call(f32[90,128]{1,0:T(8,128)S(1)} %add.7.mine, f32[90,128]{1,0:T(8,128)S(1)} %collective-permute-done.5.other, f32[90,1,256]{2,1,0:T(1,128)S(1)} %get-tuple-element.36.temp), custom_call_target="tpu_custom_call" | custom-call | flops 4194304 | bytes 2097152 | tf_op jit(solution)/shard_map/pallas_call | solution.py:361
  (2 shorter events, 0.0 us)
Async XLA Ops:
  2.3 12.3 %collective-permute-start = (f32[184,256]{1,0:T(8,128)S(1)}, f32[184,256]{1,0:T(8,128)S(1)}, u32[]{:S(2)}, u32[]{:S(2)}) collective-permute-start(f32[184,256]{1,0:T(8,128)S(1)} %get-tuple-element.23.fields), channel_id=1, source_target_pairs={{5,1},{7,3},{0,4},{9,5},{2,6},{11,7},{4,8},{13,9},{6,10},{15,11},{... | collective-permute-start | bytes 565256 | tf_op jit(solution)/shard_map/ppermute | solution.py:315
  7.2 9.6 %collective-permute-start.1 = (f32[184,256]{1,0:T(8,128)S(1)}, f32[184,256]{1,0:T(8,128)S(1)}, u32[]{:S(2)}, u32[]{:S(2)}) collective-permute-start(f32[184,256]{1,0:T(8,128)S(1)} %get-tuple-element.23.fields), channel_id=1, source_target_pairs={{9,1},{11,3},{13,5},{15,7},{0,8},{17,9},{2,10},{19,11},{4,12},{21,... | collective-permute-start | bytes 565256 | tf_op jit(solution)/shard_map/ppermute | solution.py:315
  10.7 11.2 %all-to-all-start = ((f32[8,32,128]{2,1,0:T(8,128)}), f32[8,32,128]{2,1,0:T(8,128)S(1)}, u32[]{:S(2)}, u32[]{:S(2)}) async-start(f32[8,32,128]{2,1,0:T(8,128)} %get-tuple-element.28), calls=%async_computation | async-start | bytes 262144 | tf_op jit(solution)/shard_map/all_to_all | solution.py:302
  17.5 4.7 %collective-permute-start.2 = (f32[184,256]{1,0:T(8,128)}, f32[184,256]{1,0:T(8,128)S(1)}, u32[]{:S(2)}, u32[]{:S(2)}) collective-permute-start(f32[184,256]{1,0:T(8,128)} %get-tuple-element.27), channel_id=1, source_target_pairs={{0,1},{1,0},{2,3},{3,2},{4,5},{5,4},{6,7},{7,6},{8,9},{9,8},{10,11... | collective-permute-start | bytes 565256 | tf_op jit(solution)/shard_map/ppermute | solution.py:318
  23.8 1.6 %collective-permute-start.3 = (f32[90,128]{1,0:T(8,128)S(1)}, f32[90,128]{1,0:T(8,128)S(1)}, u32[]{:S(2)}, u32[]{:S(2)}) collective-permute-start(f32[90,128]{1,0:T(8,128)S(1)} %get-tuple-element.39), channel_id=1, source_target_pairs={{0,1},{1,0},{2,3},{3,2},{4,5},{5,4},{6,7},{7,6},{8,9},{9,8},{10,11... | collective-permute-start | bytes 138248 | tf_op jit(solution)/shard_map/ppermute | solution.py:318
  25.4 4.2 %collective-permute-start.4 = (f32[90,128]{1,0:T(8,128)S(1)}, f32[90,128]{1,0:T(8,128)S(1)}, u32[]{:S(2)}, u32[]{:S(2)}) collective-permute-start(f32[90,128]{1,0:T(8,128)S(1)} %add.6), channel_id=1, source_target_pairs={{0,2},{1,3},{2,0},{3,1},{4,6},{5,7},{6,4},{7,5},{8,10},{9,11},{10,... | collective-permute-start | bytes 138248 | tf_op jit(solution)/shard_map/ppermute | solution.py:318
  29.7 1.3 %collective-permute-start.5 = (f32[90,128]{1,0:T(8,128)S(1)}, f32[90,128]{1,0:T(8,128)S(1)}, u32[]{:S(2)}, u32[]{:S(2)}) collective-permute-start(f32[90,128]{1,0:T(8,128)S(1)} %add.7.mine), channel_id=1, source_target_pairs={{0,1},{1,0},{2,3},{3,2},{4,5},{5,4},{6,7},{7,6},{8,9},{9,8},{10,11... | collective-permute-start | bytes 138248 | tf_op jit(solution)/shard_map/ppermute | solution.py:318
